TPU v7x, 768 devices: a whole 4x8x12 slice. The times are simulated.
768 devices in a mesh: dp: 24 (over y, z_hi), ctx: 32 (over z_lo, x, core).
Axes of the slice: x: 4, y: 8, z: 12 (z_hi: 3, z_lo: 4; z = z_hi * 4 + z_lo), core: 2. Of those that a mesh axis runs over, the one named last changes fastest.
Arguments:
- query_raw: bfloat16 [24, 4096, 2560], P('dp', 'ctx'), may hold values from -6 to 6
- key_raw: bfloat16 [24, 4096, 2560], P('dp', 'ctx'), may hold values from -6 to 6
- value_rows: bfloat16 [24, 4096, 2560], P('dp', 'ctx'), may hold values from -6 to 6
- out_grad: bfloat16 [24, 4096, 2560], P('dp', 'ctx'), may hold values from -6 to 6
- query_gain: float32 [2560], replicated, may hold values from 0.1 to 1.9
- key_gain: float32 [2560], replicated, may hold values from 0.1 to 1.9
Outputs:
- query_grad: bfloat16 [24, 4096, 2560], P('dp', 'ctx')
- key_grad: bfloat16 [24, 4096, 2560], P('dp', 'ctx')
- value_grad: bfloat16 [24, 4096, 2560], P('dp', 'ctx')
- gain_grads: float32 [2, 2560], replicated
All inputs are finite; a program needn't handle non-finite values.
Results may differ from a plain program's by a relative error of at most 0.011.
Values may be sent and summed in bfloat16 or wider, within the bound.
A program may use at most 32 MiB of HBM per device.

v0:
```python
import jax
import jax.numpy as jnp
from jax import lax
from jax.sharding import PartitionSpec as P

HEADS = 20
HEAD_DIM = 128


NORM_EPS = 1e-06


def padded(block, sides, width):
    for axis, dim in sides:
        count = lax.axis_size(axis)
        forward = [(i, i + 1) for i in range(count - 1)]
        backward = [(target, source) for source, target in forward]
        low = lax.ppermute(
            lax.slice_in_dim(block, block.shape[dim] - width, None, axis=dim), axis, forward
        )
        high = lax.ppermute(lax.slice_in_dim(block, 0, width, axis=dim), axis, backward)
        block = jnp.concatenate([low, block, high], axis=dim)
    return block


def shifted(block, axis, distance):
    devices = range(lax.axis_size(axis))
    route = [(i - distance, i) for i in devices if i - distance in devices]
    return lax.ppermute(block, axis, route)


def normalize(raw_rows, gain_row):
    widened = raw_rows.astype(jnp.float32)
    factor = lax.rsqrt(jnp.mean(widened * widened, axis=-1, keepdims=True) + NORM_EPS)
    return ((widened * factor * gain_row).astype(jnp.bfloat16), factor)


def norm_backward(raw_rows, factor, gain_row, upstream):
    widened = raw_rows.astype(jnp.float32)
    scaled = upstream * gain_row
    inner = jnp.mean(widened * scaled, axis=-1, keepdims=True)
    raw_grad = factor * scaled - widened * (factor * factor * factor) * inner
    gain_part = jnp.sum(upstream * widened * factor, axis=0)
    return (raw_grad.astype(jnp.bfloat16), gain_part)


def split_heads(matrix):
    return matrix.reshape(matrix.shape[0], HEADS, HEAD_DIM)


def tile_pass(query_rows, key_rows, value_rows, grad_rows, valid_keys):
    score_scale = HEAD_DIM ** (-0.5)
    query_heads = split_heads(query_rows)
    key_heads = split_heads(key_rows)
    value_heads = split_heads(value_rows)
    grad_heads = split_heads(grad_rows)
    scores = (
        jnp.einsum("qhd,khd->hqk", query_heads, key_heads, preferred_element_type=jnp.float32)
        * score_scale
    )
    scores = jnp.where(valid_keys[None, None, :], scores, -1e30)
    row_max = jnp.max(scores, axis=-1, keepdims=True)
    exponents = jnp.exp(scores - row_max)
    row_sum = jnp.sum(exponents, axis=-1, keepdims=True)
    attn_probs = exponents / row_sum
    probs_half = attn_probs.astype(jnp.bfloat16)
    attn_out = jnp.einsum(
        "hqk,khd->qhd", probs_half, value_heads, preferred_element_type=jnp.float32
    )
    row_delta = jnp.sum(grad_heads.astype(jnp.float32) * attn_out, axis=-1)
    grad_probs = jnp.einsum(
        "qhd,khd->hqk", grad_heads, value_heads, preferred_element_type=jnp.float32
    )
    grad_scores = (attn_probs * (grad_probs - jnp.transpose(row_delta)[:, :, None])).astype(
        jnp.bfloat16
    )
    query_grad = (
        jnp.einsum("hqk,khd->qhd", grad_scores, key_heads, preferred_element_type=jnp.float32)
        * score_scale
    )
    key_terms = (
        jnp.einsum("hqk,qhd->khd", grad_scores, query_heads, preferred_element_type=jnp.float32)
        * score_scale
    ).astype(jnp.bfloat16)
    value_terms = jnp.einsum(
        "hqk,qhd->khd", probs_half, grad_heads, preferred_element_type=jnp.float32
    ).astype(jnp.bfloat16)
    log_total = jnp.transpose((row_max + jnp.log(row_sum))[:, :, 0])
    flat_width = HEADS * HEAD_DIM
    return (
        query_grad.reshape(query_rows.shape[0], flat_width),
        key_terms.reshape(key_rows.shape[0], flat_width),
        value_terms.reshape(key_rows.shape[0], flat_width),
        log_total,
        row_delta,
    )


def per_device(query_raw, key_raw, value_rows, out_grad, query_gain, key_gain):
    tile_rows = query_raw.shape[1]
    margin = tile_rows // 4
    ctx_count = lax.axis_size("ctx")
    position = lax.axis_index("ctx")
    query_norm, query_factor = normalize(query_raw[0], query_gain)
    key_norm, key_factor = normalize(key_raw[0], key_gain)
    own_values = value_rows[0]
    own_grads = out_grad[0]
    key_window = padded(jnp.stack([key_norm, own_values]), (("ctx", 1),), margin)
    slot_ids = jnp.arange(tile_rows + 2 * margin, dtype=jnp.int32)
    valid_keys = jnp.logical_not(
        (slot_ids < margin) & (position == 0)
        | (slot_ids >= margin + tile_rows) & (position == ctx_count - 1)
    )
    query_grad, key_terms, value_terms, log_total, row_delta = tile_pass(
        query_norm, key_window[0], key_window[1], own_grads, valid_keys
    )
    key_sum = key_terms[margin : margin + tile_rows].astype(jnp.float32)
    value_sum = value_terms[margin : margin + tile_rows].astype(jnp.float32)
    edge_pad = ((0, tile_rows - margin), (0, 0))
    tail_pad = ((tile_rows - margin, 0), (0, 0))
    upper_slot = jnp.stack([key_terms[margin + tile_rows :], value_terms[margin + tile_rows :]])
    lower_slot = jnp.stack([key_terms[:margin], value_terms[:margin]])
    from_lower = shifted(upper_slot, "ctx", 1)
    from_upper = shifted(lower_slot, "ctx", -1)
    key_sum = (
        key_sum
        + jnp.pad(from_lower[0].astype(jnp.float32), edge_pad)
        + jnp.pad(from_upper[0].astype(jnp.float32), tail_pad)
    )
    value_sum = (
        value_sum
        + jnp.pad(from_lower[1].astype(jnp.float32), edge_pad)
        + jnp.pad(from_upper[1].astype(jnp.float32), tail_pad)
    )
    query_raw_grad, query_gain_part = norm_backward(
        query_raw[0], query_factor, query_gain, query_grad
    )
    key_raw_grad, key_gain_part = norm_backward(key_raw[0], key_factor, key_gain, key_sum)
    gain_sums = lax.psum((query_gain_part, key_gain_part), ("dp", "ctx"))
    return (
        query_raw_grad[None],
        key_raw_grad[None],
        value_sum.astype(jnp.bfloat16)[None],
        jnp.stack([gain_sums[0], gain_sums[1]]),
    )


def solution(mesh):
    placed = (
        P("dp", "ctx", None),
        P("dp", "ctx", None),
        P("dp", "ctx", None),
        P("dp", "ctx", None),
        P(),
        P(),
    )
    return jax.shard_map(
        per_device,
        mesh=mesh,
        in_specs=placed,
        out_specs=(P("dp", "ctx", None), P("dp", "ctx", None), P("dp", "ctx", None), P()),
        check_vma=False,
    )
```

profile of v0, /device:TPU:1, one launch (start us, length us, event | category | flops | bytes accessed | tf_op | source)
XLA Modules:
  0.0 216.8 jit_solution(14049038231058915619)
XLA Ops:
  3.3 1.5 slice_maximum_fusion
  4.8 2.3 %copy.49 = bf16[2,32,2560]{2,1,0:T(8,128)(2,1)} copy(bf16[2,32,2560]{1,2,0:T(8,128)(2,1)} %get-tuple-element.19) | data formatting | bytes 655360 | tf_op jit(solution)/shard_map/slice | solution.py:21
  7.1 12.4 %collective-permute-start.1 = (bf16[2,32,2560]{2,1,0:T(8,128)(2,1)}, bf16[2,32,2560]{2,1,0:T(8,128)(2,1)}, u32[]{:S(2)}, u32[]{:S(2)}) collective-permute-start(bf16[2,32,2560]{2,1,0:T(8,128)(2,1)} %copy.49), channel_id=1, source_target_pairs={{1,0},{2,1},{3,2},{4,3},{5,4},{6,5},{7,6},{8,7},{9,8},{10,9},{11,1... | collective-permute-start | bytes 983048 | tf_op jit(solution)/shard_map/ppermute | solution.py:21
  20.6 1.9 collective-permute-start
  23.0 2.2 copy.57
  25.2 1.6 collective-permute-done
  26.9 2.3 %copy.50 = bf16[2,32,2560]{1,2,0:T(8,128)(2,1)} copy(bf16[2,32,2560]{2,1,0:T(8,128)(2,1)} %collective-permute-done) | data formatting | bytes 655360 | tf_op jit(solution)/shard_map/ppermute | solution.py:18
  29.1 2.3 %copy.51 = bf16[2,32,2560]{1,2,0:T(8,128)(2,1)} copy(bf16[2,32,2560]{2,1,0:T(8,128)(2,1)} %collective-permute-done.1) | data formatting | bytes 655360 | tf_op jit(solution)/shard_map/ppermute | solution.py:21
  31.4 3.3 %pad_maximum_fusion = bf16[2,192,2560]{1,2,0:T(8,128)(2,1)S(1)} fusion(bf16[2,32,2560]{1,2,0:T(8,128)(2,1)} %copy.51, bf16[1,128,2560]{1,2,0:T(8,128)(2,1)S(1)} %copy.47, bf16[1,128,2560]{1,2,0:T(8,128)(2,1)S(1)} %copy-done.5, bf16[2,32,2560]{1,2,0:T(8,128)(2,1)} %copy.50), kind=kLoop, calls=%fused_computation.1 | loop fusion | flops 7864320 | bytes 3932160 | tf_op jit(solution)/shard_map/concatenate | solution.py:22
  36.4 1.9 fusion.42
  38.3 3.5 %fusion.8 = bf16[192,20,128]{2,0,1:T(8,128)(2,1)} fusion(bf16[128,20,128]{0,2,1:T(8,128)(2,1)} %bitcast.115, f32[20,128]{1,0:T(8,128)S(1)} %get-tuple-element.32, f32[20,128,192]{1,2,0:T(8,128)} %copy-done.3, pred[192]{0:T(512)(128)(4,1)S(1)} %or_not_fusion), kind=kOutput, calls=%fused_computation.18 | convolution fusion | flops 128780992 | bytes 3614912 | tf_op jit(solution)/shard_map/hqk,qhd->khd/dot_general | solution.py:85
  41.8 2.7 %fusion.26 = f32[128,20]{0,1:T(8,128)S(1)} fusion(bf16[192,20,128]{0,2,1:T(8,128)(2,1)S(1)} %bitcast.113, bf16[128,20,128]{0,2,1:T(8,128)(2,1)} %bitcast.116, f32[20,128]{1,0:T(8,128)S(1)} %get-tuple-element.32, f32[20,128,192]{1,2,0:T(8,128)} %copy-done.3, pred[192]{0:T(512)(128)(4,1)S(1)} %or_not_fusion), kind=kOutput, calls=%fused_computation.45 | convolution fusion | flops 129269952 | bytes 3625152 | tf_op jit(solution)/shard_map/hqk,khd->qhd/dot_general | solution.py:67
  44.4 2.5 %fusion.1 = bf16[20,128,192]{1,2,0:T(8,128)(2,1)S(1)} fusion(bf16[192,20,128]{0,2,1:T(8,128)(2,1)S(1)} %bitcast.114, bf16[128,20,128]{0,2,1:T(8,128)(2,1)} %bitcast.117, f32[20,128]{1,0:T(8,128)S(1)} %bitcast.122, f32[20,128,192]{1,2,0:T(8,128)} %get-tuple-element.33, f32[20,128]{1,0:T(8,128)S(1)} %get-tuple-element.32), kind=kOutput, calls=%fused_computation.3 | convolution fusion | flops 127795200 | bytes 4608000 | tf_op jit(solution)/shard_map/qhd,khd->hqk/dot_general | solution.py:71
  53.3 1.7 copy.65
  58.6 2.8 %copy.73 = f32[128,20,128]{0,2,1:T(8,128)} copy(f32[128,20,128]{2,0,1:T(8,128)} %slice_convert_fusion) | data formatting | bytes 2621440 | tf_op jit(solution)/shard_map/convert_element_type | solution.py:118
  61.4 1.7 pad_maximum_fusion.2
  63.1 4.6 %collective-permute-start.2 = (bf16[2,32,2560]{2,1,0:T(8,128)(2,1)}, bf16[2,32,2560]{2,1,0:T(8,128)(2,1)}, u32[]{:S(2)}, u32[]{:S(2)}) collective-permute-start(bf16[2,32,2560]{2,1,0:T(8,128)(2,1)} %pad_maximum_fusion.2), channel_id=1, source_target_pairs={{0,1},{1,2},{2,3},{3,4},{4,5},{5,6},{6,7},{7,8},{8,9},{9,10},{10,1... | collective-permute-start | bytes 983048 | tf_op jit(solution)/shard_map/ppermute | solution.py:29
  67.6 1.5 copy.63
  69.1 1.7 fusion.25
  70.9 1.5 copy.62
  72.3 2.9 %subtract_convert_fusion = bf16[1,128,2560]{2,1,0:T(8,128)(2,1)} fusion(f32[1,128,2560]{2,1,0:T(8,128)} %copy.62, bf16[1,128,2560]{2,1,0:T(8,128)(2,1)} %param.6, f32[128]{0:T(128)S(1)} %broadcast_multiply_fusion.1, f32[128]{0:T(128)S(1)} %get-tuple-element.30, f32[2560]{0:T(1024)S(1)} %copy-done.12, f32[128]{0:T(128)S(1)} %get-tuple-element.31), kind=kLoop, calls=%fused_computation.43 | loop fusion | flops 2293760 | bytes 2633216 | tf_op jit(solution)/shard_map/convert_element_type | solution.py:44
  76.0 1.9 collective-permute-start.3
  77.9 1.7 fusion.40
  79.6 2.1 copy.90
  81.7 3.0 %collective-permute-done.3 = bf16[2,32,2560]{2,1,0:T(8,128)(2,1)} collective-permute-done((bf16[2,32,2560]{2,1,0:T(8,128)(2,1)}, bf16[2,32,2560]{2,1,0:T(8,128)(2,1)}, u32[]{:S(2)}, u32[]{:S(2)}) %collective-permute-start.3) | collective-permute-done | bytes 327712 | tf_op jit(solution)/shard_map/ppermute | solution.py:29
  84.7 1.8 fusion.41
  86.5 2.0 copy.91
  88.4 2.6 %fusion.20 = bf16[128,2560]{0,1:T(8,128)(2,1)} fusion(f32[128,20,128]{0,2,1:T(8,128)S(1)} %copy-done.6, bf16[32,2560]{0,1:T(8,128)(2,1)} %bitcast.111, bf16[32,2560]{0,1:T(8,128)(2,1)} %bitcast.110), kind=kLoop, calls=%fused_computation.33 | loop fusion | flops 1638400 | bytes 2293760 | tf_op jit(solution)/shard_map/convert_element_type | solution.py:143
  91.1 2.2 copy.77
  95.9 1.5 fusion.31
  97.4 2.2 copy.76
  99.6 116.6 %all-reduce.4 = (f32[1,2560]{1,0:T(1,128)S(1)}, f32[1,2560]{1,0:T(1,128)S(1)}) all-reduce(f32[1,2560]{1,0:T(1,128)S(1)} %stack.39, f32[1,2560]{1,0:T(1,128)S(1)} %bitcast.121), channel_id=1, replica_groups=mesh['dp'=24,'ctx'=32] {'dp','ctx'}, use_global_device_ids=true, to_apply=%region_10.11 | all-reduce | flops 5120 | bytes 40960 | tf_op jit(solution)/shard_map/psum | solution.py:139
  (65 shorter events, 19.8 us)
Async XLA Ops:
  0.6 1.9 copy-start.11
  2.1 0.7 copy-start.13
  3.2 1.6 copy-start.4
  4.8 17.8 %copy-start.2 = (bf16[1,128,2560]{2,1,0:T(8,128)(2,1)S(1)}, bf16[1,128,2560]{2,1,0:T(8,128)(2,1)}, u32[]{:S(2)}) copy-start(bf16[1,128,2560]{2,1,0:T(8,128)(2,1)} %param.6) | copy-start | bytes 1966084
  7.1 22.1 %collective-permute-start.1 = (bf16[2,32,2560]{2,1,0:T(8,128)(2,1)}, bf16[2,32,2560]{2,1,0:T(8,128)(2,1)}, u32[]{:S(2)}, u32[]{:S(2)}) collective-permute-start(bf16[2,32,2560]{2,1,0:T(8,128)(2,1)} %copy.49), channel_id=1, source_target_pairs={{1,0},{2,1},{3,2},{4,3},{5,4},{6,5},{7,6},{8,7},{9,8},{10,9},{11,1... | collective-permute-start | bytes 983048 | tf_op jit(solution)/shard_map/ppermute | solution.py:21
  20.6 6.2 %collective-permute-start = (bf16[2,32,2560]{2,1,0:T(8,128)(2,1)}, bf16[2,32,2560]{2,1,0:T(8,128)(2,1)}, u32[]{:S(2)}, u32[]{:S(2)}) collective-permute-start(bf16[2,32,2560]{2,1,0:T(8,128)(2,1)} %copy.48), channel_id=1, source_target_pairs={{0,1},{1,2},{2,3},{3,4},{4,5},{5,6},{6,7},{7,8},{8,9},{9,10},{10,1... | collective-permute-start | bytes 983048 | tf_op jit(solution)/shard_map/ppermute | solution.py:18
  25.2 6.2 %copy-start.5 = (bf16[1,128,2560]{1,2,0:T(8,128)(2,1)S(1)}, bf16[1,128,2560]{1,2,0:T(8,128)(2,1)}, u32[]{:S(2)}) copy-start(bf16[1,128,2560]{1,2,0:T(8,128)(2,1)} %copy-done.4) | copy-start | bytes 1966084
  34.7 0.7 copy-start.12
  34.9 1.5 copy-start
  36.4 1.9 copy-start.3
  44.4 2.5 %copy-start.1 = (bf16[1,192,2560]{1,2,0:T(8,128)(2,1)S(1)}, bf16[1,192,2560]{1,2,0:T(8,128)(2,1)}, u32[]{:S(2)}) copy-start(bf16[1,192,2560]{1,2,0:T(8,128)(2,1)} %copy-done) | copy-start | bytes 2949124
  48.2 1.5 copy-start.7
  58.6 2.8 %copy-start.10 = (bf16[1,32,2560]{2,1,0:T(8,128)(2,1)S(1)}, bf16[1,32,2560]{2,1,0:T(8,128)(2,1)}, u32[]{:S(2)}) copy-start(bf16[1,32,2560]{2,1,0:T(8,128)(2,1)} %stack.32) | copy-start | bytes 491524
  63.1 14.9 %collective-permute-start.2 = (bf16[2,32,2560]{2,1,0:T(8,128)(2,1)}, bf16[2,32,2560]{2,1,0:T(8,128)(2,1)}, u32[]{:S(2)}, u32[]{:S(2)}) collective-permute-start(bf16[2,32,2560]{2,1,0:T(8,128)(2,1)} %pad_maximum_fusion.2), channel_id=1, source_target_pairs={{0,1},{1,2},{2,3},{3,4},{4,5},{5,6},{6,7},{7,8},{8,9},{9,10},{10,1... | collective-permute-start | bytes 983048 | tf_op jit(solution)/shard_map/ppermute | solution.py:29
  72.3 2.9 %copy-start.8 = (bf16[1,32,2560]{2,1,0:T(8,128)(2,1)S(1)}, bf16[1,32,2560]{2,1,0:T(8,128)(2,1)}, u32[]{:S(2)}) copy-start(bf16[1,32,2560]{2,1,0:T(8,128)(2,1)} %stack.35) | copy-start | bytes 491524
  72.3 2.9 %copy-start.9 = (bf16[1,32,2560]{2,1,0:T(8,128)(2,1)S(1)}, bf16[1,32,2560]{2,1,0:T(8,128)(2,1)}, u32[]{:S(2)}) copy-start(bf16[1,32,2560]{2,1,0:T(8,128)(2,1)} %stack.36) | copy-start | bytes 491524
  76.0 8.7 %collective-permute-start.3 = (bf16[2,32,2560]{2,1,0:T(8,128)(2,1)}, bf16[2,32,2560]{2,1,0:T(8,128)(2,1)}, u32[]{:S(2)}, u32[]{:S(2)}) collective-permute-start(bf16[2,32,2560]{2,1,0:T(8,128)(2,1)} %pad_maximum_fusion.3), channel_id=1, source_target_pairs={{1,0},{2,1},{3,2},{4,3},{5,4},{6,5},{7,6},{8,7},{9,8},{10,9},{11,1... | collective-permute-start | bytes 983048 | tf_op jit(solution)/shard_map/ppermute | solution.py:29
  79.6 8.8 %copy-start.6 = (f32[128,20,128]{0,2,1:T(8,128)S(1)}, f32[128,20,128]{0,2,1:T(8,128)}, u32[]{:S(2)}) copy-start(f32[128,20,128]{0,2,1:T(8,128)} %copy.73) | copy-start | bytes 3932164
where the time goes:
time: 218 us; the launch traced here: 217 us
  blocking collectives  117 us (54%)
  local copies, waits for them, and re-layouts  40.1 us (18%)
  other arithmetic  23 us (11%)
  starting transfers between devices  20.7 us (9%)
  matrix products  10.8 us (5%)
  waiting for transfers between devices  4.63 us (2%)
    psum x1, blocking collectives, per_device(): gain_sums = lax.psum((query_gain_part, key_gain_part), ('dp', 'ctx'))  117 us
    unnamed x38, local copies, waits for them, and re-layouts  14.7 us
    ppermute x1, starting transfers between devices, padded(): lax.ppermute(lax.slice_in_dim(block, 0, width, axis=dim), axis, backward)  12.4 us
    ppermute x2, starting transfers between devices, shifted(): return lax.ppermute(block, axis, route)  6.46 us
  transfers between devices with their start and end apart: 4, of which 2 were waited for; matrix products, arithmetic and copies ran while one was open for 8% of the time, Pallas kernels for 0%

commit v1 on v0

--- a/solution.py
+++ b/solution.py
@@ -21,6 +21,52 @@
         high = lax.ppermute(lax.slice_in_dim(block, 0, width, axis=dim), axis, backward)
         block = jnp.concatenate([low, block, high], axis=dim)
     return block
+
+
+AXIS_PARTS = {"ctx": (4, 4, 2), "dp": (8, 3)}
+
+
+def part_steps(axis):
+    total = lax.axis_size(axis)
+    sizes = AXIS_PARTS[axis]
+    stride = total
+    steps = []
+    for size in sizes:
+        stride //= size
+        steps.append((size, stride))
+    return total, steps
+
+
+def partner_pairs(total, size, stride, move):
+    pairs = []
+    for i in range(total):
+        c = (i // stride) % size
+        pairs.append((i, i + (move(c) - c) * stride))
+    return pairs
+
+
+def axis_sum(x, axis):
+    total, steps = part_steps(axis)
+    for size, stride in reversed(steps):
+        if size & (size - 1):
+            acc = x
+            for k in range(1, size):
+                acc = acc + lax.ppermute(
+                    x, axis, partner_pairs(total, size, stride, lambda c: (c + k) % size)
+                )
+            x = acc
+        else:
+            d = 1
+            while d < size:
+                x = x + lax.ppermute(
+                    x, axis, partner_pairs(total, size, stride, lambda c: c ^ d)
+                )
+                d *= 2
+    return x
+
+
+def mesh_sum(x):
+    return axis_sum(axis_sum(x, "dp"), "ctx")
 
 
 def shifted(block, axis, distance):
@@ -136,12 +182,12 @@
         query_raw[0], query_factor, query_gain, query_grad
     )
     key_raw_grad, key_gain_part = norm_backward(key_raw[0], key_factor, key_gain, key_sum)
-    gain_sums = lax.psum((query_gain_part, key_gain_part), ("dp", "ctx"))
+    gain_sums = mesh_sum(jnp.stack([query_gain_part, key_gain_part]))
     return (
         query_raw_grad[None],
         key_raw_grad[None],
         value_sum.astype(jnp.bfloat16)[None],
-        jnp.stack([gain_sums[0], gain_sums[1]]),
+        gain_sums,
     )
 
 

time: 218 us -> 156 us (0.72)
  blocking collectives: 117 us -> 0 us
  starting transfers between devices: 20.7 us -> 69.6 us
  waiting for transfers between devices: 4.63 us -> 12.6 us
  local copies, waits for them, and re-layouts: 40.1 us -> 36.7 us
    psum x1 -> x0, blocking collectives: 117 us -> none  [per_device(): gain_sums = lax.psum((query_gain_part, key_gain_part), ('dp', 'ctx'))]
    ppermute x0 -> x10, starting transfers between devices: none -> 48.9 us  [the longest x8 39.7 us: axis_sum(): lax.ppermute(x, axis, partner_pairs(total, size, stride, lambda c: c ^ d))]
    ppermute x0 -> x10, waiting for transfers between devices: none -> 7 us  [the longest x2 5.84 us: axis_sum(): lax.ppermute(x, axis, partner_pairs(total, size, stride, lambda c: (c + k...]
    unnamed x38 -> x40, local copies, waits for them, and re-layouts: 14.7 us -> 12.3 us
    convert_element_type x1, other arithmetic: 2.63 us -> 0.36 us  [per_device(): value_sum.astype(jnp.bfloat16)[None]]
  transfers between devices with their start and end apart: 4 -> 14, of which waited for: 2 -> 5; matrix products, arithmetic and copies ran while one was open for 8% -> 18% of each run, Pallas kernels for 0% -> 0%
where the time goes in v1:
time: 156 us; the launch traced here: 154 us
  starting transfers between devices  69.6 us (45%)
  local copies, waits for them, and re-layouts  36.7 us (24%)
  other arithmetic  23.1 us (15%)
  waiting for transfers between devices  12.6 us (8%)
  matrix products  10.8 us (7%)
    ppermute x8, starting transfers between devices, axis_sum(): lax.ppermute(x, axis, partner_pairs(total, size, stride, lambda c: c ^ d))  39.7 us
    ppermute x1, starting transfers between devices, padded(): lax.ppermute(lax.slice_in_dim(block, 0, width, axis=dim), axis, backward)  12.4 us
    unnamed x40, local copies, waits for them, and re-layouts  12.3 us
    ppermute x2, starting transfers between devices, axis_sum(): lax.ppermute(x, axis, partner_pairs(total, size, stride, lambda c: (c + k...  9.19 us
    ppermute x2, starting transfers between devices, shifted(): return lax.ppermute(block, axis, route)  6.48 us
    ppermute x2, waiting for transfers between devices, axis_sum(): lax.ppermute(x, axis, partner_pairs(total, size, stride, lambda c: (c + k...  5.84 us
    ppermute x2, waiting for transfers between devices, shifted(): return lax.ppermute(block, axis, route)  3.92 us
    dot_general x1, matrix products, tile_pass(): jnp.einsum('hqk,qhd->khd', probs_half, grad_heads, preferred_element_type...  3.5 us
  transfers between devices with their start and end apart: 14, of which 5 were waited for; matrix products, arithmetic and copies ran while one was open for 18% of the time, Pallas kernels for 0%

profile of v1, /device:TPU:1, one launch (start us, length us, event | category | flops | bytes accessed | tf_op | source)
XLA Modules:
  0.0 154.0 jit_solution(1593575668750624552)
XLA Ops:
  5.3 2.3 %copy.49 = bf16[2,32,2560]{2,1,0:T(8,128)(2,1)} copy(bf16[2,32,2560]{1,2,0:T(8,128)(2,1)} %get-tuple-element.17) | data formatting | bytes 655360 | tf_op jit(solution)/shard_map/slice | solution.py:21
  7.6 12.4 %collective-permute-start.1 = (bf16[2,32,2560]{2,1,0:T(8,128)(2,1)}, bf16[2,32,2560]{2,1,0:T(8,128)(2,1)}, u32[]{:S(2)}, u32[]{:S(2)}) collective-permute-start(bf16[2,32,2560]{2,1,0:T(8,128)(2,1)} %copy.49), channel_id=1, source_target_pairs={{1,0},{2,1},{3,2},{4,3},{5,4},{6,5},{7,6},{8,7},{9,8},{10,9},{11,1... | collective-permute-start | bytes 983048 | tf_op jit(solution)/shard_map/ppermute | solution.py:21
  21.2 1.9 %collective-permute-start = (bf16[2,32,2560]{2,1,0:T(8,128)(2,1)}, bf16[2,32,2560]{2,1,0:T(8,128)(2,1)}, u32[]{:S(2)}, u32[]{:S(2)}) collective-permute-start(bf16[2,32,2560]{2,1,0:T(8,128)(2,1)} %copy.48), channel_id=1, source_target_pairs={{0,1},{1,2},{2,3},{3,4},{4,5},{5,6},{6,7},{7,8},{8,9},{9,10},{10,1... | collective-permute-start | bytes 983048 | tf_op jit(solution)/shard_map/ppermute | solution.py:18
  23.6 2.2 %copy.57 = bf16[1,128,2560]{1,2,0:T(8,128)(2,1)} copy(bf16[1,128,2560]{2,1,0:T(8,128)(2,1)} %param.9) | data formatting | bytes 1310720 | tf_op args[3]
  27.4 2.3 %copy.50 = bf16[2,32,2560]{1,2,0:T(8,128)(2,1)} copy(bf16[2,32,2560]{2,1,0:T(8,128)(2,1)} %collective-permute-done) | data formatting | bytes 655360 | tf_op jit(solution)/shard_map/ppermute | solution.py:18
  29.7 2.3 %copy.51 = bf16[2,32,2560]{1,2,0:T(8,128)(2,1)} copy(bf16[2,32,2560]{2,1,0:T(8,128)(2,1)} %collective-permute-done.1) | data formatting | bytes 655360 | tf_op jit(solution)/shard_map/ppermute | solution.py:21
  31.9 3.3 %pad_maximum_fusion = bf16[2,192,2560]{1,2,0:T(8,128)(2,1)S(1)} fusion(bf16[2,32,2560]{1,2,0:T(8,128)(2,1)} %copy.51, bf16[1,128,2560]{1,2,0:T(8,128)(2,1)S(1)} %copy.47, bf16[1,128,2560]{1,2,0:T(8,128)(2,1)S(1)} %copy-done.5, bf16[2,32,2560]{1,2,0:T(8,128)(2,1)} %copy.50), kind=kLoop, calls=%fused_computation.1 | loop fusion | flops 7864320 | bytes 3932160 | tf_op jit(solution)/shard_map/concatenate | solution.py:22
  36.9 1.9 %fusion.42 = (f32[20,128]{1,0:T(8,128)S(1)}, f32[20,128,192]{1,2,0:T(8,128)}) fusion(f32[20,128,192]{1,2,0:T(8,128)S(1)} %fusion.32, pred[192]{0:T(512)(128)(4,1)S(1)} %or_not_fusion), kind=kOutput, calls=%fused_computation.74 | output fusion | flops 1966271 | bytes 3942592 | tf_op jit(solution)/shard_map/sub | solution.py:109
  38.8 3.5 %fusion.8 = bf16[192,20,128]{2,0,1:T(8,128)(2,1)} fusion(bf16[128,20,128]{0,2,1:T(8,128)(2,1)} %bitcast.115, f32[20,128]{1,0:T(8,128)S(1)} %get-tuple-element.30, f32[20,128,192]{1,2,0:T(8,128)} %copy-done.3, pred[192]{0:T(512)(128)(4,1)S(1)} %or_not_fusion), kind=kOutput, calls=%fused_computation.18 | convolution fusion | flops 128780992 | bytes 3614912 | tf_op jit(solution)/shard_map/hqk,qhd->khd/dot_general | solution.py:131
  42.3 2.7 %fusion.26 = f32[128,20]{0,1:T(8,128)S(1)} fusion(bf16[192,20,128]{0,2,1:T(8,128)(2,1)S(1)} %bitcast.113, bf16[128,20,128]{0,2,1:T(8,128)(2,1)} %bitcast.116, f32[20,128]{1,0:T(8,128)S(1)} %get-tuple-element.30, f32[20,128,192]{1,2,0:T(8,128)} %copy-done.3, pred[192]{0:T(512)(128)(4,1)S(1)} %or_not_fusion), kind=kOutput, calls=%fused_computation.45 | convolution fusion | flops 129269952 | bytes 3625152 | tf_op jit(solution)/shard_map/hqk,khd->qhd/dot_general | solution.py:113
  45.0 2.5 %fusion.1 = bf16[20,128,192]{1,2,0:T(8,128)(2,1)S(1)} fusion(bf16[192,20,128]{0,2,1:T(8,128)(2,1)S(1)} %bitcast.114, bf16[128,20,128]{0,2,1:T(8,128)(2,1)} %bitcast.117, f32[20,128]{1,0:T(8,128)S(1)} %bitcast.123, f32[20,128,192]{1,2,0:T(8,128)} %get-tuple-element.31, f32[20,128]{1,0:T(8,128)S(1)} %get-tuple-element.30), kind=kOutput, calls=%fused_computation.3 | convolution fusion | flops 127795200 | bytes 4608000 | tf_op jit(solution)/shard_map/qhd,khd->hqk/dot_general | solution.py:117
  58.7 4.4 %collective-permute-start.2 = (bf16[2,32,2560]{2,1,0:T(8,128)(2,1)S(1)}, bf16[2,32,2560]{2,1,0:T(8,128)(2,1)S(1)}, u32[]{:S(2)}, u32[]{:S(2)}) collective-permute-start(bf16[2,32,2560]{2,1,0:T(8,128)(2,1)S(1)} %pad_maximum_fusion.2), channel_id=1, source_target_pairs={{0,1},{1,2},{2,3},{3,4},{4,5},{5,6},{6,7},{7,8},{8,9},{9,10},{10,1... | collective-permute-start | bytes 983048 | tf_op jit(solution)/shard_map/ppermute | solution.py:75
  63.1 1.8 %pad_maximum_fusion.3 = bf16[2,32,2560]{2,1,0:T(8,128)(2,1)} fusion(bf16[1,32,2560]{2,1,0:T(8,128)(2,1)} %stack.36, bf16[1,32,2560]{2,1,0:T(8,128)(2,1)} %stack.35), kind=kLoop, calls=%fused_computation.55 | loop fusion | flops 163840 | bytes 655360 | tf_op jit(solution)/shard_map/stack | solution.py:168
  64.9 2.1 %collective-permute-start.3 = (bf16[2,32,2560]{2,1,0:T(8,128)(2,1)}, bf16[2,32,2560]{2,1,0:T(8,128)(2,1)}, u32[]{:S(2)}, u32[]{:S(2)}) collective-permute-start(bf16[2,32,2560]{2,1,0:T(8,128)(2,1)} %pad_maximum_fusion.3), channel_id=1, source_target_pairs={{1,0},{2,1},{3,2},{4,3},{5,4},{6,5},{7,6},{8,7},{9,8},{10,9},{11,1... | collective-permute-start | bytes 983048 | tf_op jit(solution)/shard_map/ppermute | solution.py:75
  67.8 2.0 %copy.88 = bf16[1,32,2560]{1,2,0:T(8,128)(2,1)} copy(bf16[1,32,2560]{2,1,0:T(8,128)(2,1)} %get-tuple-element.23) | data formatting | bytes 327680
  69.8 3.8 %collective-permute-done.3 = bf16[2,32,2560]{2,1,0:T(8,128)(2,1)} collective-permute-done((bf16[2,32,2560]{2,1,0:T(8,128)(2,1)}, bf16[2,32,2560]{2,1,0:T(8,128)(2,1)}, u32[]{:S(2)}, u32[]{:S(2)}) %collective-permute-start.3) | collective-permute-done | bytes 327712 | tf_op jit(solution)/shard_map/ppermute | solution.py:75
  75.3 2.0 %copy.89 = bf16[1,32,2560]{1,2,0:T(8,128)(2,1)} copy(bf16[1,32,2560]{2,1,0:T(8,128)(2,1)} %get-tuple-element.25) | data formatting | bytes 327680
  77.3 2.4 %fusion.16 = (f32[2560]{0:T(1024)S(1)}, f32[128]{0:T(128)S(1)}) fusion(bf16[1,128,2560]{1,2,0:T(8,128)(2,1)S(1)} %copy.46, f32[128]{0:T(128)S(1)} %get-tuple-element.27, bf16[32,2560]{0,1:T(8,128)(2,1)} %bitcast.108, bf16[32,2560]{0,1:T(8,128)(2,1)} %bitcast.106, f32[128,20,128]{0,2,1:T(8,128)S(1)} %copy.65, f32[2560]{0:T(1024)S(1)} %copy-done.13), kind=kLoop, calls=%fused_computation.26 | loop fusion | flops 3601792 | bytes 2315264 | tf_op jit(solution)/shard_map/reduce_sum | solution.py:89
  79.7 6.4 %collective-permute-start.5 = (f32[2,2560]{1,0:T(2,128)S(1)}, f32[2,2560]{1,0:T(2,128)S(1)}, u32[]{:S(2)}, u32[]{:S(2)}) collective-permute-start(f32[2,2560]{1,0:T(2,128)S(1)} %pad_maximum_fusion.4), channel_id=1, source_target_pairs={{0,64},{32,0},{64,32},{96,160},{128,96},{160,128},{192,256},{224,1... | collective-permute-start | bytes 61448 | tf_op jit(solution)/shard_map/ppermute | solution.py:54
  86.1 2.8 %collective-permute-start.4 = (f32[2,2560]{1,0:T(2,128)S(1)}, f32[2,2560]{1,0:T(2,128)S(1)}, u32[]{:S(2)}, u32[]{:S(2)}) collective-permute-start(f32[2,2560]{1,0:T(2,128)S(1)} %pad_maximum_fusion.4), channel_id=1, source_target_pairs={{0,32},{32,64},{64,0},{96,128},{128,160},{160,96},{192,224},{224,2... | collective-permute-start | bytes 61448 | tf_op jit(solution)/shard_map/ppermute | solution.py:54
  88.9 5.8 %collective-permute-done.4 = f32[2,2560]{1,0:T(2,128)S(1)} collective-permute-done((f32[2,2560]{1,0:T(2,128)S(1)}, f32[2,2560]{1,0:T(2,128)S(1)}, u32[]{:S(2)}, u32[]{:S(2)}) %collective-permute-start.4) | collective-permute-done | bytes 20512 | tf_op jit(solution)/shard_map/ppermute | solution.py:54
  94.8 3.2 %collective-permute-start.6 = (f32[2,2560]{1,0:T(2,128)S(1)}, f32[2,2560]{1,0:T(2,128)S(1)}, u32[]{:S(2)}, u32[]{:S(2)}) collective-permute-start(f32[2,2560]{1,0:T(2,128)S(1)} %add_add_fusion), channel_id=1, source_target_pairs={{0,96},{32,128},{64,160},{96,0},{128,32},{160,64},{192,288},{224,3... | collective-permute-start | bytes 61448 | tf_op jit(solution)/shard_map/ppermute | solution.py:61
  99.5 4.2 %collective-permute-start.7 = (f32[2,2560]{1,0:T(2,128)S(1)}, f32[2,2560]{1,0:T(2,128)S(1)}, u32[]{:S(2)}, u32[]{:S(2)}) collective-permute-start(f32[2,2560]{1,0:T(2,128)S(1)} %add.80), channel_id=1, source_target_pairs={{0,192},{32,224},{64,256},{96,288},{128,320},{160,352},{192,0},{22... | collective-permute-start | bytes 61448 | tf_op jit(solution)/shard_map/ppermute | solution.py:61
  103.7 1.7 %fusion.25 = f32[128]{0:T(128)S(1)} fusion(f32[128,2560]{1,0:T(8,128)} %copy.63, bf16[1,128,2560]{2,1,0:T(8,128)(2,1)} %param.6, f32[2560]{0:T(1024)S(1)} %copy-done.12), kind=kLoop, calls=%fused_computation.42 | loop fusion | flops 1310592 | bytes 1976832 | tf_op jit(solution)/shard_map/reduce_sum | solution.py:87
  105.5 7.0 %collective-permute-start.8 = (f32[2,2560]{1,0:T(2,128)S(1)}, f32[2,2560]{1,0:T(2,128)S(1)}, u32[]{:S(2)}, u32[]{:S(2)}) collective-permute-start(f32[2,2560]{1,0:T(2,128)S(1)} %add.81), channel_id=1, source_target_pairs={{0,384},{32,416},{64,448},{96,480},{128,512},{160,544},{192,576},{... | collective-permute-start | bytes 61448 | tf_op jit(solution)/shard_map/ppermute | solution.py:61
  114.0 1.9 %collective-permute-start.9 = (f32[2,2560]{1,0:T(2,128)S(1)}, f32[2,2560]{1,0:T(2,128)S(1)}, u32[]{:S(2)}, u32[]{:S(2)}) collective-permute-start(f32[2,2560]{1,0:T(2,128)S(1)} %add.82), channel_id=1, source_target_pairs={{0,1},{1,0},{2,3},{3,2},{4,5},{5,4},{6,7},{7,6},{8,9},{9,8},{10,11... | collective-permute-start | bytes 61448 | tf_op jit(solution)/shard_map/ppermute | solution.py:61
  115.9 2.9 %subtract_convert_fusion = bf16[1,128,2560]{2,1,0:T(8,128)(2,1)} fusion(f32[1,128,2560]{2,1,0:T(8,128)} %copy.62, bf16[1,128,2560]{2,1,0:T(8,128)(2,1)} %param.6, f32[128]{0:T(128)S(1)} %broadcast_multiply_fusion.1, f32[128]{0:T(128)S(1)} %get-tuple-element.28, f32[2560]{0:T(1024)S(1)} %copy-done.12, f32[128]{0:T(128)S(1)} %get-tuple-element.29), kind=kLoop, calls=%fused_computation.43 | loop fusion | flops 2293760 | bytes 2633216 | tf_op jit(solution)/shard_map/convert_element_type | solution.py:90
  118.9 5.9 %collective-permute-start.10 = (f32[2,2560]{1,0:T(2,128)S(1)}, f32[2,2560]{1,0:T(2,128)S(1)}, u32[]{:S(2)}, u32[]{:S(2)}) collective-permute-start(f32[2,2560]{1,0:T(2,128)S(1)} %add.83), channel_id=1, source_target_pairs={{0,2},{1,3},{2,0},{3,1},{4,6},{5,7},{6,4},{7,5},{8,10},{9,11},{10,... | collective-permute-start | bytes 61448 | tf_op jit(solution)/shard_map/ppermute | solution.py:61
  126.0 2.9 %copy.73 = f32[128,20,128]{0,2,1:T(8,128)} copy(f32[128,20,128]{2,0,1:T(8,128)} %slice_convert_fusion) | data formatting | bytes 2621440 | tf_op jit(solution)/shard_map/convert_element_type | solution.py:164
  128.9 8.1 %collective-permute-start.11 = (f32[2,2560]{1,0:T(2,128)S(1)}, f32[2,2560]{1,0:T(2,128)S(1)}, u32[]{:S(2)}, u32[]{:S(2)}) collective-permute-start(f32[2,2560]{1,0:T(2,128)S(1)} %add.84), channel_id=1, source_target_pairs={{0,4},{1,5},{2,6},{3,7},{4,0},{5,1},{6,2},{7,3},{8,12},{9,13},{10,... | collective-permute-start | bytes 61448 | tf_op jit(solution)/shard_map/ppermute | solution.py:61
  138.2 5.0 %collective-permute-start.12 = (f32[2,2560]{1,0:T(2,128)S(1)}, f32[2,2560]{1,0:T(2,128)S(1)}, u32[]{:S(2)}, u32[]{:S(2)}) collective-permute-start(f32[2,2560]{1,0:T(2,128)S(1)} %add.85), channel_id=1, source_target_pairs={{0,8},{1,9},{2,10},{3,11},{4,12},{5,13},{6,14},{7,15},{8,0},{9,1},... | collective-permute-start | bytes 61448 | tf_op jit(solution)/shard_map/ppermute | solution.py:61
  146.4 4.4 %collective-permute-start.13 = (f32[2,2560]{1,0:T(2,128)S(1)}, f32[2,2560]{1,0:T(2,128)S(1)}, u32[]{:S(2)}, u32[]{:S(2)}) collective-permute-start(f32[2,2560]{1,0:T(2,128)S(1)} %add.86), channel_id=1, source_target_pairs={{0,16},{1,17},{2,18},{3,19},{4,20},{5,21},{6,22},{7,23},{8,24},{9,... | collective-permute-start | bytes 61448 | tf_op jit(solution)/shard_map/ppermute | solution.py:61
  (95 shorter events, 35.2 us)
Async XLA Ops:
  0.6 2.4 %copy-start.11 = (bf16[1,128,2560]{2,1,0:T(8,128)(2,1)S(1)}, bf16[1,128,2560]{2,1,0:T(8,128)(2,1)}, u32[]{:S(2)}) copy-start(bf16[1,128,2560]{2,1,0:T(8,128)(2,1)} %param.8) | copy-start | bytes 1966084
  2.1 1.2 copy-start.13
  3.8 1.6 %copy-start.4 = (bf16[1,128,2560]{1,2,0:T(8,128)(2,1)}, bf16[1,128,2560]{1,2,0:T(8,128)(2,1)S(1)}, u32[]{:S(2)}) copy-start(bf16[1,128,2560]{1,2,0:T(8,128)(2,1)S(1)} %fusion.18) | copy-start | bytes 1966084
  5.3 17.8 %copy-start.2 = (bf16[1,128,2560]{2,1,0:T(8,128)(2,1)S(1)}, bf16[1,128,2560]{2,1,0:T(8,128)(2,1)}, u32[]{:S(2)}) copy-start(bf16[1,128,2560]{2,1,0:T(8,128)(2,1)} %param.6) | copy-start | bytes 1966084
  7.6 22.1 %collective-permute-start.1 = (bf16[2,32,2560]{2,1,0:T(8,128)(2,1)}, bf16[2,32,2560]{2,1,0:T(8,128)(2,1)}, u32[]{:S(2)}, u32[]{:S(2)}) collective-permute-start(bf16[2,32,2560]{2,1,0:T(8,128)(2,1)} %copy.49), channel_id=1, source_target_pairs={{1,0},{2,1},{3,2},{4,3},{5,4},{6,5},{7,6},{8,7},{9,8},{10,9},{11,1... | collective-permute-start | bytes 983048 | tf_op jit(solution)/shard_map/ppermute | solution.py:21
  21.2 6.2 %collective-permute-start = (bf16[2,32,2560]{2,1,0:T(8,128)(2,1)}, bf16[2,32,2560]{2,1,0:T(8,128)(2,1)}, u32[]{:S(2)}, u32[]{:S(2)}) collective-permute-start(bf16[2,32,2560]{2,1,0:T(8,128)(2,1)} %copy.48), channel_id=1, source_target_pairs={{0,1},{1,2},{2,3},{3,4},{4,5},{5,6},{6,7},{7,8},{8,9},{9,10},{10,1... | collective-permute-start | bytes 983048 | tf_op jit(solution)/shard_map/ppermute | solution.py:18
  25.8 6.2 %copy-start.5 = (bf16[1,128,2560]{1,2,0:T(8,128)(2,1)S(1)}, bf16[1,128,2560]{1,2,0:T(8,128)(2,1)}, u32[]{:S(2)}) copy-start(bf16[1,128,2560]{1,2,0:T(8,128)(2,1)} %copy-done.4) | copy-start | bytes 1966084
  35.2 0.7 copy-start.12
  35.4 1.5 copy-start
  36.9 1.9 %copy-start.3 = (f32[20,128,192]{1,2,0:T(8,128)}, f32[20,128,192]{1,2,0:T(8,128)S(1)}, u32[]{:S(2)}) copy-start(f32[20,128,192]{1,2,0:T(8,128)S(1)} %fusion.32) | copy-start | bytes 5898244
  45.0 2.5 %copy-start.1 = (bf16[1,192,2560]{1,2,0:T(8,128)(2,1)S(1)}, bf16[1,192,2560]{1,2,0:T(8,128)(2,1)}, u32[]{:S(2)}) copy-start(bf16[1,192,2560]{1,2,0:T(8,128)(2,1)} %copy-done) | copy-start | bytes 2949124
  58.7 8.4 %collective-permute-start.2 = (bf16[2,32,2560]{2,1,0:T(8,128)(2,1)S(1)}, bf16[2,32,2560]{2,1,0:T(8,128)(2,1)S(1)}, u32[]{:S(2)}, u32[]{:S(2)}) collective-permute-start(bf16[2,32,2560]{2,1,0:T(8,128)(2,1)S(1)} %pad_maximum_fusion.2), channel_id=1, source_target_pairs={{0,1},{1,2},{2,3},{3,4},{4,5},{5,6},{6,7},{7,8},{8,9},{9,10},{10,1... | collective-permute-start | bytes 983048 | tf_op jit(solution)/shard_map/ppermute | solution.py:75
  64.9 8.7 %collective-permute-start.3 = (bf16[2,32,2560]{2,1,0:T(8,128)(2,1)}, bf16[2,32,2560]{2,1,0:T(8,128)(2,1)}, u32[]{:S(2)}, u32[]{:S(2)}) collective-permute-start(bf16[2,32,2560]{2,1,0:T(8,128)(2,1)} %pad_maximum_fusion.3), channel_id=1, source_target_pairs={{1,0},{2,1},{3,2},{4,3},{5,4},{6,5},{7,6},{8,7},{9,8},{10,9},{11,1... | collective-permute-start | bytes 983048 | tf_op jit(solution)/shard_map/ppermute | solution.py:75
  79.7 9.2 %collective-permute-start.5 = (f32[2,2560]{1,0:T(2,128)S(1)}, f32[2,2560]{1,0:T(2,128)S(1)}, u32[]{:S(2)}, u32[]{:S(2)}) collective-permute-start(f32[2,2560]{1,0:T(2,128)S(1)} %pad_maximum_fusion.4), channel_id=1, source_target_pairs={{0,64},{32,0},{64,32},{96,160},{128,96},{160,128},{192,256},{224,1... | collective-permute-start | bytes 61448 | tf_op jit(solution)/shard_map/ppermute | solution.py:54
  86.1 8.7 %collective-permute-start.4 = (f32[2,2560]{1,0:T(2,128)S(1)}, f32[2,2560]{1,0:T(2,128)S(1)}, u32[]{:S(2)}, u32[]{:S(2)}) collective-permute-start(f32[2,2560]{1,0:T(2,128)S(1)} %pad_maximum_fusion.4), channel_id=1, source_target_pairs={{0,32},{32,64},{64,0},{96,128},{128,160},{160,96},{192,224},{224,2... | collective-permute-start | bytes 61448 | tf_op jit(solution)/shard_map/ppermute | solution.py:54
  94.8 4.7 %collective-permute-start.6 = (f32[2,2560]{1,0:T(2,128)S(1)}, f32[2,2560]{1,0:T(2,128)S(1)}, u32[]{:S(2)}, u32[]{:S(2)}) collective-permute-start(f32[2,2560]{1,0:T(2,128)S(1)} %add_add_fusion), channel_id=1, source_target_pairs={{0,96},{32,128},{64,160},{96,0},{128,32},{160,64},{192,288},{224,3... | collective-permute-start | bytes 61448 | tf_op jit(solution)/shard_map/ppermute | solution.py:61
  99.5 6.0 %collective-permute-start.7 = (f32[2,2560]{1,0:T(2,128)S(1)}, f32[2,2560]{1,0:T(2,128)S(1)}, u32[]{:S(2)}, u32[]{:S(2)}) collective-permute-start(f32[2,2560]{1,0:T(2,128)S(1)} %add.80), channel_id=1, source_target_pairs={{0,192},{32,224},{64,256},{96,288},{128,320},{160,352},{192,0},{22... | collective-permute-start | bytes 61448 | tf_op jit(solution)/shard_map/ppermute | solution.py:61
  105.5 8.5 %collective-permute-start.8 = (f32[2,2560]{1,0:T(2,128)S(1)}, f32[2,2560]{1,0:T(2,128)S(1)}, u32[]{:S(2)}, u32[]{:S(2)}) collective-permute-start(f32[2,2560]{1,0:T(2,128)S(1)} %add.81), channel_id=1, source_target_pairs={{0,384},{32,416},{64,448},{96,480},{128,512},{160,544},{192,576},{... | collective-permute-start | bytes 61448 | tf_op jit(solution)/shard_map/ppermute | solution.py:61
  114.0 4.9 %collective-permute-start.9 = (f32[2,2560]{1,0:T(2,128)S(1)}, f32[2,2560]{1,0:T(2,128)S(1)}, u32[]{:S(2)}, u32[]{:S(2)}) collective-permute-start(f32[2,2560]{1,0:T(2,128)S(1)} %add.82), channel_id=1, source_target_pairs={{0,1},{1,0},{2,3},{3,2},{4,5},{5,4},{6,7},{7,6},{8,9},{9,8},{10,11... | collective-permute-start | bytes 61448 | tf_op jit(solution)/shard_map/ppermute | solution.py:61
  115.9 8.9 %copy-start.10 = (bf16[192,20,128]{2,0,1:T(8,128)(2,1)S(1)}, bf16[192,20,128]{2,0,1:T(8,128)(2,1)}, u32[]{:S(2)}) copy-start(bf16[192,20,128]{2,0,1:T(8,128)(2,1)} %fusion.8) | copy-start | bytes 2949124
  118.9 10.1 %collective-permute-start.10 = (f32[2,2560]{1,0:T(2,128)S(1)}, f32[2,2560]{1,0:T(2,128)S(1)}, u32[]{:S(2)}, u32[]{:S(2)}) collective-permute-start(f32[2,2560]{1,0:T(2,128)S(1)} %add.83), channel_id=1, source_target_pairs={{0,2},{1,3},{2,0},{3,1},{4,6},{5,7},{6,4},{7,5},{8,10},{9,11},{10,... | collective-permute-start | bytes 61448 | tf_op jit(solution)/shard_map/ppermute | solution.py:61
  126.0 17.2 %copy-start.6 = (bf16[1,32,2560]{1,2,0:T(8,128)(2,1)S(1)}, bf16[1,32,2560]{1,2,0:T(8,128)(2,1)}, u32[]{:S(2)}) copy-start(bf16[1,32,2560]{1,2,0:T(8,128)(2,1)} %copy.88) | copy-start | bytes 491524
  126.0 17.2 %copy-start.7 = (bf16[1,32,2560]{1,2,0:T(8,128)(2,1)S(1)}, bf16[1,32,2560]{1,2,0:T(8,128)(2,1)}, u32[]{:S(2)}) copy-start(bf16[1,32,2560]{1,2,0:T(8,128)(2,1)} %copy.89) | copy-start | bytes 491524
  126.0 17.2 %copy-start.14 = (f32[128]{0:T(128)S(1)}, f32[128]{0:T(128)}, u32[]{:S(2)}) copy-start(f32[128]{0:T(128)} %get-tuple-element.26) | copy-start | bytes 1540
  128.9 9.2 %collective-permute-start.11 = (f32[2,2560]{1,0:T(2,128)S(1)}, f32[2,2560]{1,0:T(2,128)S(1)}, u32[]{:S(2)}, u32[]{:S(2)}) collective-permute-start(f32[2,2560]{1,0:T(2,128)S(1)} %add.84), channel_id=1, source_target_pairs={{0,4},{1,5},{2,6},{3,7},{4,0},{5,1},{6,2},{7,3},{8,12},{9,13},{10,... | collective-permute-start | bytes 61448 | tf_op jit(solution)/shard_map/ppermute | solution.py:61
  138.2 8.1 %collective-permute-start.12 = (f32[2,2560]{1,0:T(2,128)S(1)}, f32[2,2560]{1,0:T(2,128)S(1)}, u32[]{:S(2)}, u32[]{:S(2)}) collective-permute-start(f32[2,2560]{1,0:T(2,128)S(1)} %add.85), channel_id=1, source_target_pairs={{0,8},{1,9},{2,10},{3,11},{4,12},{5,13},{6,14},{7,15},{8,0},{9,1},... | collective-permute-start | bytes 61448 | tf_op jit(solution)/shard_map/ppermute | solution.py:61
  144.7 6.1 %copy-start.8 = (f32[128,20,128]{0,2,1:T(8,128)S(1)}, f32[128,20,128]{0,2,1:T(8,128)}, u32[]{:S(2)}) copy-start(f32[128,20,128]{0,2,1:T(8,128)} %copy.73) | copy-start | bytes 3932164
  146.4 7.0 %collective-permute-start.13 = (f32[2,2560]{1,0:T(2,128)S(1)}, f32[2,2560]{1,0:T(2,128)S(1)}, u32[]{:S(2)}, u32[]{:S(2)}) collective-permute-start(f32[2,2560]{1,0:T(2,128)S(1)} %add.86), channel_id=1, source_target_pairs={{0,16},{1,17},{2,18},{3,19},{4,20},{5,21},{6,22},{7,23},{8,24},{9,... | collective-permute-start | bytes 61448 | tf_op jit(solution)/shard_map/ppermute | solution.py:61
  151.1 1.1 copy-start.9

commit v2 on v0

--- a/solution.py
+++ b/solution.py
@@ -1,6 +1,10 @@
+import functools
+
 import jax
 import jax.numpy as jnp
 from jax import lax
+from jax.experimental import pallas as pl
+from jax.experimental.pallas import tpu as pltpu
 from jax.sharding import PartitionSpec as P
 
 HEADS = 20
@@ -21,6 +25,99 @@
         high = lax.ppermute(lax.slice_in_dim(block, 0, width, axis=dim), axis, backward)
         block = jnp.concatenate([low, block, high], axis=dim)
     return block
+
+
+AXIS_PARTS = {"ctx": (4, 4, 2), "dp": (8, 3)}
+SUM_ORDER = (("dp", 1), ("dp", 0), ("ctx", 0), ("ctx", 1), ("ctx", 2))
+
+
+def sum_plan():
+    plan = []
+    for axis, part in SUM_ORDER:
+        sizes = AXIS_PARTS[axis]
+        stride = 1
+        for later in sizes[part + 1:]:
+            stride *= later
+        size = sizes[part]
+        if size & (size - 1):
+            plan.append((axis, size, stride, "ring"))
+        else:
+            d = 1
+            while d < size:
+                plan.append((axis, size, stride, d))
+                d *= 2
+    return plan
+
+
+def moved(index, size, stride, new_coord_fn):
+    c = (index // stride) % size
+    return index + (new_coord_fn(c) - c) * stride
+
+
+def step_partners(kind, size, stride, index):
+    if kind == "ring":
+        return [moved(index, size, stride, lambda c, k=k: (c + k) % size) for k in range(1, size)]
+    d = kind
+    return [moved(index, size, stride, lambda c: c + d - 2 * d * ((c // d) % 2))]
+
+
+def sum_kernel(plan, x_ref, o_ref, acc, slots, send_sem, recv_sem):
+    here = {"dp": lax.axis_index("dp"), "ctx": lax.axis_index("ctx")}
+    steps = []
+    for axis, size, stride, kind in plan:
+        ids = []
+        for other in step_partners(kind, size, stride, here[axis]):
+            dev = dict(here)
+            dev[axis] = other
+            ids.append((dev["dp"], dev["ctx"]))
+        steps.append(ids)
+    barrier = pltpu.get_barrier_semaphore()
+    count = 0
+    for ids in steps:
+        for dev in ids:
+            pl.semaphore_signal(barrier, inc=1, device_id=dev, device_id_type=pl.DeviceIdType.MESH)
+            count += 1
+    pl.semaphore_wait(barrier, count)
+    acc[0] = x_ref[...]
+    slot = 0
+    for s, ids in enumerate(steps):
+        copies = []
+        for dev in ids:
+            copy = pltpu.make_async_remote_copy(
+                src_ref=acc.at[s],
+                dst_ref=slots.at[slot],
+                send_sem=send_sem.at[slot],
+                recv_sem=recv_sem.at[slot],
+                device_id=dev,
+                device_id_type=pl.DeviceIdType.MESH,
+            )
+            copy.start()
+            copies.append((copy, slot))
+            slot += 1
+        total = acc[s]
+        for copy, used in copies:
+            copy.wait()
+            total = total + slots[used]
+        acc[s + 1] = total
+    o_ref[...] = acc[len(steps)]
+
+
+def mesh_sum(x):
+    plan = sum_plan()
+    n_slots = sum(len(step_partners(k, s, st, 0)) for _, s, st, k in plan)
+    return pl.pallas_call(
+        functools.partial(sum_kernel, plan),
+        out_shape=jax.ShapeDtypeStruct(x.shape, x.dtype),
+        in_specs=[pl.BlockSpec(memory_space=pltpu.VMEM)],
+        out_specs=pl.BlockSpec(memory_space=pltpu.VMEM),
+        scratch_shapes=[
+            pltpu.VMEM((len(plan) + 1,) + x.shape, x.dtype),
+            pltpu.VMEM((n_slots,) + x.shape, x.dtype),
+            pltpu.SemaphoreType.DMA((n_slots,)),
+            pltpu.SemaphoreType.DMA((n_slots,)),
+        ],
+        compiler_params=pltpu.CompilerParams(collective_id=7, has_side_effects=True),
+    )(x)
 
 
 def shifted(block, axis, distance):
@@ -136,12 +233,12 @@
         query_raw[0], query_factor, query_gain, query_grad
     )
     key_raw_grad, key_gain_part = norm_backward(key_raw[0], key_factor, key_gain, key_sum)
-    gain_sums = lax.psum((query_gain_part, key_gain_part), ("dp", "ctx"))
+    gain_sums = mesh_sum(jnp.stack([query_gain_part, key_gain_part]))
     return (
         query_raw_grad[None],
         key_raw_grad[None],
         value_sum.astype(jnp.bfloat16)[None],
-        jnp.stack([gain_sums[0], gain_sums[1]]),
+        gain_sums,
     )
 
 

time: 218 us -> 145 us (0.67)
  blocking collectives: 117 us -> 0 us
  Pallas kernels: 0 us -> 43.1 us
    psum x1 -> x0, blocking collectives: 117 us -> none  [per_device(): gain_sums = lax.psum((query_gain_part, key_gain_part), ('dp', 'ctx'))]
    pallas_call x0 -> x1, Pallas kernels: none -> 43.1 us  [mesh_sum(): pl.pallas_call(functools.partial(sum_kernel, plan), out_shape=jax.ShapeDt...]
    unnamed x38 -> x41, local copies, waits for them, and re-layouts: 14.7 us -> 15.4 us
  transfers between devices with their start and end apart: 4 -> 4, of which waited for: 2 -> 2; matrix products, arithmetic and copies ran while one was open for 8% -> 13% of each run, Pallas kernels for 0% -> 0%
where the time goes in v2:
time: 145 us; the launch traced here: 144 us
  Pallas kernels  43.1 us (30%)
  local copies, waits for them, and re-layouts  40.7 us (28%)
  other arithmetic  23 us (16%)
  starting transfers between devices  20.7 us (14%)
  matrix products  10.8 us (7%)
  waiting for transfers between devices  4.63 us (3%)
    pallas_call x1, Pallas kernels, mesh_sum(): pl.pallas_call(functools.partial(sum_kernel, plan), out_shape=jax.ShapeDt...  43.1 us
    unnamed x41, local copies, waits for them, and re-layouts  15.4 us
    ppermute x1, starting transfers between devices, padded(): lax.ppermute(lax.slice_in_dim(block, 0, width, axis=dim), axis, backward)  12.4 us
    ppermute x2, starting transfers between devices, shifted(): return lax.ppermute(block, axis, route)  6.46 us
    dot_general x1, matrix products, tile_pass(): jnp.einsum('hqk,qhd->khd', probs_half, grad_heads, preferred_element_type...  3.5 us
    concatenate x1, other arithmetic, padded(): block = jnp.concatenate([low, block, high], axis=dim)  3.31 us
    ppermute x2, waiting for transfers between devices, shifted(): return lax.ppermute(block, axis, route)  2.99 us
    reshape x2, local copies, waits for them, and re-layouts, tile_pass(): query_grad.reshape(query_rows.shape[0], flat_width)  2.97 us
  transfers between devices with their start and end apart: 4, of which 2 were waited for; matrix products, arithmetic and copies ran while one was open for 13% of the time, Pallas kernels for 0%

profile of v2, /device:TPU:1, one launch (start us, length us, event | category | flops | bytes accessed | tf_op | source)
XLA Modules:
  0.0 143.9 jit_solution(1916194734164506984)
XLA Ops:
  3.3 1.5 %slice_maximum_fusion = (bf16[2,32,2560]{1,2,0:T(8,128)(2,1)S(1)}, bf16[2,32,2560]{1,2,0:T(8,128)(2,1)}) fusion(bf16[1,128,2560]{1,2,0:T(8,128)(2,1)S(1)} %copy.47, bf16[1,128,2560]{1,2,0:T(8,128)(2,1)S(1)} %fusion.18), kind=kLoop, calls=%fused_computation.30 | loop fusion | flops 1310720 | bytes 1966080 | tf_op jit(solution)/shard_map/stack | solution.py:205
  4.8 2.3 %copy.49 = bf16[2,32,2560]{2,1,0:T(8,128)(2,1)} copy(bf16[2,32,2560]{1,2,0:T(8,128)(2,1)} %get-tuple-element.17) | data formatting | bytes 655360 | tf_op jit(solution)/shard_map/slice | solution.py:25
  7.1 12.4 %collective-permute-start.1 = (bf16[2,32,2560]{2,1,0:T(8,128)(2,1)}, bf16[2,32,2560]{2,1,0:T(8,128)(2,1)}, u32[]{:S(2)}, u32[]{:S(2)}) collective-permute-start(bf16[2,32,2560]{2,1,0:T(8,128)(2,1)} %copy.49), channel_id=1, source_target_pairs={{1,0},{2,1},{3,2},{4,3},{5,4},{6,5},{7,6},{8,7},{9,8},{10,9},{11,1... | collective-permute-start | bytes 983048 | tf_op jit(solution)/shard_map/ppermute | solution.py:25
  20.6 1.9 %collective-permute-start = (bf16[2,32,2560]{2,1,0:T(8,128)(2,1)}, bf16[2,32,2560]{2,1,0:T(8,128)(2,1)}, u32[]{:S(2)}, u32[]{:S(2)}) collective-permute-start(bf16[2,32,2560]{2,1,0:T(8,128)(2,1)} %copy.48), channel_id=1, source_target_pairs={{0,1},{1,2},{2,3},{3,4},{4,5},{5,6},{6,7},{7,8},{8,9},{9,10},{10,1... | collective-permute-start | bytes 983048 | tf_op jit(solution)/shard_map/ppermute | solution.py:22
  23.0 2.2 %copy.57 = bf16[1,128,2560]{1,2,0:T(8,128)(2,1)} copy(bf16[1,128,2560]{2,1,0:T(8,128)(2,1)} %param.9) | data formatting | bytes 1310720 | tf_op args[3]
  25.2 1.6 %collective-permute-done = bf16[2,32,2560]{2,1,0:T(8,128)(2,1)} collective-permute-done((bf16[2,32,2560]{2,1,0:T(8,128)(2,1)}, bf16[2,32,2560]{2,1,0:T(8,128)(2,1)}, u32[]{:S(2)}, u32[]{:S(2)}) %collective-permute-start) | collective-permute-done | bytes 327712 | tf_op jit(solution)/shard_map/ppermute | solution.py:22
  26.9 2.3 %copy.50 = bf16[2,32,2560]{1,2,0:T(8,128)(2,1)} copy(bf16[2,32,2560]{2,1,0:T(8,128)(2,1)} %collective-permute-done) | data formatting | bytes 655360 | tf_op jit(solution)/shard_map/ppermute | solution.py:22
  29.1 2.3 %copy.51 = bf16[2,32,2560]{1,2,0:T(8,128)(2,1)} copy(bf16[2,32,2560]{2,1,0:T(8,128)(2,1)} %collective-permute-done.1) | data formatting | bytes 655360 | tf_op jit(solution)/shard_map/ppermute | solution.py:25
  31.4 3.3 %pad_maximum_fusion = bf16[2,192,2560]{1,2,0:T(8,128)(2,1)S(1)} fusion(bf16[2,32,2560]{1,2,0:T(8,128)(2,1)} %copy.51, bf16[1,128,2560]{1,2,0:T(8,128)(2,1)S(1)} %copy.47, bf16[1,128,2560]{1,2,0:T(8,128)(2,1)S(1)} %copy-done.5, bf16[2,32,2560]{1,2,0:T(8,128)(2,1)} %copy.50), kind=kLoop, calls=%fused_computation.1 | loop fusion | flops 7864320 | bytes 3932160 | tf_op jit(solution)/shard_map/concatenate | solution.py:26
  36.4 1.9 %fusion.42 = (f32[20,128]{1,0:T(8,128)S(1)}, f32[20,128,192]{1,2,0:T(8,128)}) fusion(f32[20,128,192]{1,2,0:T(8,128)S(1)} %fusion.32, pred[192]{0:T(512)(128)(4,1)S(1)} %or_not_fusion), kind=kOutput, calls=%fused_computation.73 | output fusion | flops 1966271 | bytes 3942592 | tf_op jit(solution)/shard_map/sub | solution.py:160
  38.3 3.5 %fusion.8 = bf16[192,20,128]{2,0,1:T(8,128)(2,1)} fusion(bf16[128,20,128]{0,2,1:T(8,128)(2,1)} %bitcast.115, f32[20,128]{1,0:T(8,128)S(1)} %get-tuple-element.30, f32[20,128,192]{1,2,0:T(8,128)} %copy-done.3, pred[192]{0:T(512)(128)(4,1)S(1)} %or_not_fusion), kind=kOutput, calls=%fused_computation.18 | convolution fusion | flops 128780992 | bytes 3614912 | tf_op jit(solution)/shard_map/hqk,qhd->khd/dot_general | solution.py:182
  41.8 2.7 %fusion.26 = f32[128,20]{0,1:T(8,128)S(1)} fusion(bf16[192,20,128]{0,2,1:T(8,128)(2,1)S(1)} %bitcast.113, bf16[128,20,128]{0,2,1:T(8,128)(2,1)} %bitcast.116, f32[20,128]{1,0:T(8,128)S(1)} %get-tuple-element.30, f32[20,128,192]{1,2,0:T(8,128)} %copy-done.3, pred[192]{0:T(512)(128)(4,1)S(1)} %or_not_fusion), kind=kOutput, calls=%fused_computation.45 | convolution fusion | flops 129269952 | bytes 3625152 | tf_op jit(solution)/shard_map/hqk,khd->qhd/dot_general | solution.py:164
  44.4 2.5 %fusion.1 = bf16[20,128,192]{1,2,0:T(8,128)(2,1)S(1)} fusion(bf16[192,20,128]{0,2,1:T(8,128)(2,1)S(1)} %bitcast.114, bf16[128,20,128]{0,2,1:T(8,128)(2,1)} %bitcast.117, f32[20,128]{1,0:T(8,128)S(1)} %bitcast.122, f32[20,128,192]{1,2,0:T(8,128)} %get-tuple-element.31, f32[20,128]{1,0:T(8,128)S(1)} %get-tuple-element.30), kind=kOutput, calls=%fused_computation.3 | convolution fusion | flops 127795200 | bytes 4608000 | tf_op jit(solution)/shard_map/qhd,khd->hqk/dot_general | solution.py:168
  53.3 1.7 %copy.65 = f32[128,20,128]{0,2,1:T(8,128)S(1)} copy(f32[128,20,128]{2,0,1:T(8,128)} %slice_convert_fusion.1) | data formatting | bytes 2621440 | tf_op jit(solution)/shard_map/convert_element_type | solution.py:214
  58.6 2.8 %copy.73 = f32[128,20,128]{0,2,1:T(8,128)} copy(f32[128,20,128]{2,0,1:T(8,128)} %slice_convert_fusion) | data formatting | bytes 2621440 | tf_op jit(solution)/shard_map/convert_element_type | solution.py:215
  61.4 1.7 %pad_maximum_fusion.2 = bf16[2,32,2560]{2,1,0:T(8,128)(2,1)} fusion(bf16[1,32,2560]{2,1,0:T(8,128)(2,1)} %stack.33, bf16[1,32,2560]{2,1,0:T(8,128)(2,1)S(1)} %copy-done.10), kind=kLoop, calls=%fused_computation.54 | loop fusion | flops 163840 | bytes 655360 | tf_op jit(solution)/shard_map/stack | solution.py:218
  63.1 4.6 %collective-permute-start.2 = (bf16[2,32,2560]{2,1,0:T(8,128)(2,1)}, bf16[2,32,2560]{2,1,0:T(8,128)(2,1)}, u32[]{:S(2)}, u32[]{:S(2)}) collective-permute-start(bf16[2,32,2560]{2,1,0:T(8,128)(2,1)} %pad_maximum_fusion.2), channel_id=1, source_target_pairs={{0,1},{1,2},{2,3},{3,4},{4,5},{5,6},{6,7},{7,8},{8,9},{9,10},{10,1... | collective-permute-start | bytes 983048 | tf_op jit(solution)/shard_map/ppermute | solution.py:126
  67.6 1.5 %copy.63 = f32[128,2560]{1,0:T(8,128)} copy(f32[128,2560]{0,1:T(8,128)S(1)} %bitcast.102) | data formatting | bytes 2621440 | tf_op jit(solution)/shard_map/reshape | solution.py:188
  69.1 1.7 %fusion.25 = f32[128]{0:T(128)S(1)} fusion(f32[128,2560]{1,0:T(8,128)} %copy.63, bf16[1,128,2560]{2,1,0:T(8,128)(2,1)} %param.6, f32[2560]{0:T(1024)S(1)} %copy-done.12), kind=kLoop, calls=%fused_computation.42 | loop fusion | flops 1310592 | bytes 1976832 | tf_op jit(solution)/shard_map/reduce_sum | solution.py:138
  70.9 1.5 %copy.62 = f32[1,128,2560]{2,1,0:T(8,128)} copy(f32[1,128,2560]{1,2,0:T(8,128)S(1)} %bitcast.103) | data formatting | bytes 2621440 | tf_op jit(solution)/shard_map/reshape | solution.py:188
  72.3 2.9 %subtract_convert_fusion = bf16[1,128,2560]{2,1,0:T(8,128)(2,1)} fusion(f32[1,128,2560]{2,1,0:T(8,128)} %copy.62, bf16[1,128,2560]{2,1,0:T(8,128)(2,1)} %param.6, f32[128]{0:T(128)S(1)} %broadcast_multiply_fusion.1, f32[128]{0:T(128)S(1)} %get-tuple-element.28, f32[2560]{0:T(1024)S(1)} %copy-done.12, f32[128]{0:T(128)S(1)} %get-tuple-element.29), kind=kLoop, calls=%fused_computation.43 | loop fusion | flops 2293760 | bytes 2633216 | tf_op jit(solution)/shard_map/convert_element_type | solution.py:141
  76.0 1.9 %collective-permute-start.3 = (bf16[2,32,2560]{2,1,0:T(8,128)(2,1)}, bf16[2,32,2560]{2,1,0:T(8,128)(2,1)}, u32[]{:S(2)}, u32[]{:S(2)}) collective-permute-start(bf16[2,32,2560]{2,1,0:T(8,128)(2,1)} %pad_maximum_fusion.3), channel_id=1, source_target_pairs={{1,0},{2,1},{3,2},{4,3},{5,4},{6,5},{7,6},{8,7},{9,8},{10,9},{11,1... | collective-permute-start | bytes 983048 | tf_op jit(solution)/shard_map/ppermute | solution.py:126
  77.9 1.7 %fusion.40 = (bf16[1,32,2560]{2,1,0:T(8,128)(2,1)}, bf16[1,32,2560]{2,1,0:T(8,128)(2,1)S(1)}) fusion(bf16[2,32,2560]{2,1,0:T(8,128)(2,1)} %collective-permute-done.2), kind=kLoop, calls=%fused_computation.71 | loop fusion | bytes 655360 | tf_op jit(solution)/shard_map/slice | solution.py:229
  79.6 2.1 %copy.90 = bf16[1,32,2560]{1,2,0:T(8,128)(2,1)} copy(bf16[1,32,2560]{2,1,0:T(8,128)(2,1)} %get-tuple-element.22) | data formatting | bytes 327680
  81.7 3.0 %collective-permute-done.3 = bf16[2,32,2560]{2,1,0:T(8,128)(2,1)} collective-permute-done((bf16[2,32,2560]{2,1,0:T(8,128)(2,1)}, bf16[2,32,2560]{2,1,0:T(8,128)(2,1)}, u32[]{:S(2)}, u32[]{:S(2)}) %collective-permute-start.3) | collective-permute-done | bytes 327712 | tf_op jit(solution)/shard_map/ppermute | solution.py:126
  84.7 1.8 %fusion.41 = (bf16[1,32,2560]{2,1,0:T(8,128)(2,1)}, bf16[1,32,2560]{2,1,0:T(8,128)(2,1)}) fusion(bf16[2,32,2560]{2,1,0:T(8,128)(2,1)} %collective-permute-done.3), kind=kLoop, calls=%fused_computation.72 | loop fusion | bytes 655360 | tf_op jit(solution)/shard_map/slice | solution.py:230
  86.5 2.0 %copy.91 = bf16[1,32,2560]{1,2,0:T(8,128)(2,1)} copy(bf16[1,32,2560]{2,1,0:T(8,128)(2,1)} %get-tuple-element.24) | data formatting | bytes 327680
  88.4 2.6 %fusion.20 = bf16[128,2560]{0,1:T(8,128)(2,1)} fusion(f32[128,20,128]{0,2,1:T(8,128)S(1)} %copy-done.6, bf16[32,2560]{0,1:T(8,128)(2,1)} %bitcast.111, bf16[32,2560]{0,1:T(8,128)(2,1)} %bitcast.110), kind=kLoop, calls=%fused_computation.33 | loop fusion | flops 1638400 | bytes 2293760 | tf_op jit(solution)/shard_map/convert_element_type | solution.py:240
  91.1 2.2 %copy.77 = bf16[1,128,2560]{2,1,0:T(8,128)(2,1)} copy(bf16[1,128,2560]{1,2,0:T(8,128)(2,1)} %bitcast.112) | data formatting | bytes 1310720
  96.5 43.1 %shard_map.93 = f32[2,2560]{1,0:T(2,128)} custom-call(f32[2,2560]{1,0:T(2,128)} %pad_maximum_fusion.4.x_ref), custom_call_target="tpu_custom_call" | custom-call | tf_op jit(solution)/shard_map/pallas_call | solution.py:108
  139.7 1.5 %fusion.31 = bf16[1,128,2560]{1,2,0:T(8,128)(2,1)} fusion(bf16[1,128,2560]{1,2,0:T(8,128)(2,1)S(1)} %copy.46, f32[128]{0:T(128)S(1)} %broadcast_multiply_fusion, f32[128]{0:T(128)S(1)} %get-tuple-element.26, f32[2560]{0:T(1024)S(1)} %copy-done.13, f32[128]{0:T(128)S(1)} %get-tuple-element.27, bf16[32,2560]{0,1:T(8,128)(2,1)S(1)} %bitcast.109, ...), kind=kLoop, calls=%fused_computation.51 | loop fusion | flops 3604480 | bytes 2960896 | tf_op jit(solution)/shard_map/broadcast_in_dim | solution.py:239
  141.1 2.2 %copy.76 = bf16[1,128,2560]{2,1,0:T(8,128)(2,1)} copy(bf16[1,128,2560]{1,2,0:T(8,128)(2,1)} %fusion.31) | data formatting | bytes 1310720
  (68 shorter events, 20.4 us)
Async XLA Ops:
  0.6 1.9 %copy-start.11 = (bf16[1,128,2560]{2,1,0:T(8,128)(2,1)S(1)}, bf16[1,128,2560]{2,1,0:T(8,128)(2,1)}, u32[]{:S(2)}) copy-start(bf16[1,128,2560]{2,1,0:T(8,128)(2,1)} %param.8) | copy-start | bytes 1966084
  2.1 0.7 copy-start.13
  3.2 1.6 %copy-start.4 = (bf16[1,128,2560]{1,2,0:T(8,128)(2,1)}, bf16[1,128,2560]{1,2,0:T(8,128)(2,1)S(1)}, u32[]{:S(2)}) copy-start(bf16[1,128,2560]{1,2,0:T(8,128)(2,1)S(1)} %fusion.18) | copy-start | bytes 1966084
  4.8 17.8 %copy-start.2 = (bf16[1,128,2560]{2,1,0:T(8,128)(2,1)S(1)}, bf16[1,128,2560]{2,1,0:T(8,128)(2,1)}, u32[]{:S(2)}) copy-start(bf16[1,128,2560]{2,1,0:T(8,128)(2,1)} %param.6) | copy-start | bytes 1966084
  7.1 22.1 %collective-permute-start.1 = (bf16[2,32,2560]{2,1,0:T(8,128)(2,1)}, bf16[2,32,2560]{2,1,0:T(8,128)(2,1)}, u32[]{:S(2)}, u32[]{:S(2)}) collective-permute-start(bf16[2,32,2560]{2,1,0:T(8,128)(2,1)} %copy.49), channel_id=1, source_target_pairs={{1,0},{2,1},{3,2},{4,3},{5,4},{6,5},{7,6},{8,7},{9,8},{10,9},{11,1... | collective-permute-start | bytes 983048 | tf_op jit(solution)/shard_map/ppermute | solution.py:25
  20.6 6.2 %collective-permute-start = (bf16[2,32,2560]{2,1,0:T(8,128)(2,1)}, bf16[2,32,2560]{2,1,0:T(8,128)(2,1)}, u32[]{:S(2)}, u32[]{:S(2)}) collective-permute-start(bf16[2,32,2560]{2,1,0:T(8,128)(2,1)} %copy.48), channel_id=1, source_target_pairs={{0,1},{1,2},{2,3},{3,4},{4,5},{5,6},{6,7},{7,8},{8,9},{9,10},{10,1... | collective-permute-start | bytes 983048 | tf_op jit(solution)/shard_map/ppermute | solution.py:22
  25.2 6.2 %copy-start.5 = (bf16[1,128,2560]{1,2,0:T(8,128)(2,1)S(1)}, bf16[1,128,2560]{1,2,0:T(8,128)(2,1)}, u32[]{:S(2)}) copy-start(bf16[1,128,2560]{1,2,0:T(8,128)(2,1)} %copy-done.4) | copy-start | bytes 1966084
  34.7 0.7 copy-start.12
  34.9 1.5 %copy-start = (bf16[1,192,2560]{1,2,0:T(8,128)(2,1)}, bf16[1,192,2560]{1,2,0:T(8,128)(2,1)S(1)}, u32[]{:S(2)}) copy-start(bf16[1,192,2560]{1,2,0:T(8,128)(2,1)S(1)} %get-tuple-element.15) | copy-start | bytes 2949124
  36.4 1.9 %copy-start.3 = (f32[20,128,192]{1,2,0:T(8,128)}, f32[20,128,192]{1,2,0:T(8,128)S(1)}, u32[]{:S(2)}) copy-start(f32[20,128,192]{1,2,0:T(8,128)S(1)} %fusion.32) | copy-start | bytes 5898244
  44.4 2.5 %copy-start.1 = (bf16[1,192,2560]{1,2,0:T(8,128)(2,1)S(1)}, bf16[1,192,2560]{1,2,0:T(8,128)(2,1)}, u32[]{:S(2)}) copy-start(bf16[1,192,2560]{1,2,0:T(8,128)(2,1)} %copy-done) | copy-start | bytes 2949124
  48.2 1.5 %copy-start.7 = (bf16[192,20,128]{2,0,1:T(8,128)(2,1)S(1)}, bf16[192,20,128]{2,0,1:T(8,128)(2,1)}, u32[]{:S(2)}) copy-start(bf16[192,20,128]{2,0,1:T(8,128)(2,1)} %fusion.8) | copy-start | bytes 2949124
  58.6 2.8 %copy-start.10 = (bf16[1,32,2560]{2,1,0:T(8,128)(2,1)S(1)}, bf16[1,32,2560]{2,1,0:T(8,128)(2,1)}, u32[]{:S(2)}) copy-start(bf16[1,32,2560]{2,1,0:T(8,128)(2,1)} %stack.32) | copy-start | bytes 491524
  63.1 14.9 %collective-permute-start.2 = (bf16[2,32,2560]{2,1,0:T(8,128)(2,1)}, bf16[2,32,2560]{2,1,0:T(8,128)(2,1)}, u32[]{:S(2)}, u32[]{:S(2)}) collective-permute-start(bf16[2,32,2560]{2,1,0:T(8,128)(2,1)} %pad_maximum_fusion.2), channel_id=1, source_target_pairs={{0,1},{1,2},{2,3},{3,4},{4,5},{5,6},{6,7},{7,8},{8,9},{9,10},{10,1... | collective-permute-start | bytes 983048 | tf_op jit(solution)/shard_map/ppermute | solution.py:126
  72.3 2.9 %copy-start.8 = (bf16[1,32,2560]{2,1,0:T(8,128)(2,1)S(1)}, bf16[1,32,2560]{2,1,0:T(8,128)(2,1)}, u32[]{:S(2)}) copy-start(bf16[1,32,2560]{2,1,0:T(8,128)(2,1)} %stack.35) | copy-start | bytes 491524
  72.3 2.9 %copy-start.9 = (bf16[1,32,2560]{2,1,0:T(8,128)(2,1)S(1)}, bf16[1,32,2560]{2,1,0:T(8,128)(2,1)}, u32[]{:S(2)}) copy-start(bf16[1,32,2560]{2,1,0:T(8,128)(2,1)} %stack.36) | copy-start | bytes 491524
  76.0 8.7 %collective-permute-start.3 = (bf16[2,32,2560]{2,1,0:T(8,128)(2,1)}, bf16[2,32,2560]{2,1,0:T(8,128)(2,1)}, u32[]{:S(2)}, u32[]{:S(2)}) collective-permute-start(bf16[2,32,2560]{2,1,0:T(8,128)(2,1)} %pad_maximum_fusion.3), channel_id=1, source_target_pairs={{1,0},{2,1},{3,2},{4,3},{5,4},{6,5},{7,6},{8,7},{9,8},{10,9},{11,1... | collective-permute-start | bytes 983048 | tf_op jit(solution)/shard_map/ppermute | solution.py:126
  79.6 8.8 %copy-start.6 = (f32[128,20,128]{0,2,1:T(8,128)S(1)}, f32[128,20,128]{0,2,1:T(8,128)}, u32[]{:S(2)}) copy-start(f32[128,20,128]{0,2,1:T(8,128)} %copy.73) | copy-start | bytes 3932164
  141.1 2.2 %copy-start.14 = (f32[2,2560]{1,0:T(2,128)S(1)}, f32[2,2560]{1,0:T(2,128)}, u32[]{:S(2)}) copy-start(f32[2,2560]{1,0:T(2,128)} %shard_map.93) | copy-start | bytes 61444

commit v3 on v2

--- a/solution.py
+++ b/solution.py
@@ -38,14 +38,7 @@
         stride = 1
         for later in sizes[part + 1:]:
             stride *= later
-        size = sizes[part]
-        if size & (size - 1):
-            plan.append((axis, size, stride, "ring"))
-        else:
-            d = 1
-            while d < size:
-                plan.append((axis, size, stride, d))
-                d *= 2
+        plan.append((axis, sizes[part], stride, "ring"))
     return plan
 
 

time: 145 us -> 138 us (0.952)
  Pallas kernels: 43.1 us -> 36.6 us
    pallas_call x1, Pallas kernels: 43.1 us -> 36.6 us  [mesh_sum(): pl.pallas_call(functools.partial(sum_kernel, plan), out_shape=jax.ShapeDt...]
where the time goes in v3:
time: 138 us; the launch traced here: 137 us
  local copies, waits for them, and re-layouts  40.7 us (29%)
  Pallas kernels  36.6 us (27%)
  other arithmetic  23 us (17%)
  starting transfers between devices  20.7 us (15%)
  matrix products  10.8 us (8%)
  waiting for transfers between devices  4.63 us (3%)
    pallas_call x1, Pallas kernels, mesh_sum(): pl.pallas_call(functools.partial(sum_kernel, plan), out_shape=jax.ShapeDt...  36.6 us
    unnamed x41, local copies, waits for them, and re-layouts  15.4 us
    ppermute x1, starting transfers between devices, padded(): lax.ppermute(lax.slice_in_dim(block, 0, width, axis=dim), axis, backward)  12.4 us
    ppermute x2, starting transfers between devices, shifted(): return lax.ppermute(block, axis, route)  6.46 us
    dot_general x1, matrix products, tile_pass(): jnp.einsum('hqk,qhd->khd', probs_half, grad_heads, preferred_element_type...  3.5 us
    concatenate x1, other arithmetic, padded(): block = jnp.concatenate([low, block, high], axis=dim)  3.31 us
    ppermute x2, waiting for transfers between devices, shifted(): return lax.ppermute(block, axis, route)  2.99 us
    reshape x2, local copies, waits for them, and re-layouts, tile_pass(): query_grad.reshape(query_rows.shape[0], flat_width)  2.97 us
  transfers between devices with their start and end apart: 4, of which 2 were waited for; matrix products, arithmetic and copies ran while one was open for 13% of the time, Pallas kernels for 0%

profile of v3, /device:TPU:1, one launch (start us, length us, event | category | flops | bytes accessed | tf_op | source)
XLA Modules:
  0.0 137.4 jit_solution(17347426197257044353)
XLA Ops:
  3.3 1.5 %slice_maximum_fusion = (bf16[2,32,2560]{1,2,0:T(8,128)(2,1)S(1)}, bf16[2,32,2560]{1,2,0:T(8,128)(2,1)}) fusion(bf16[1,128,2560]{1,2,0:T(8,128)(2,1)S(1)} %copy.47, bf16[1,128,2560]{1,2,0:T(8,128)(2,1)S(1)} %fusion.18), kind=kLoop, calls=%fused_computation.30 | loop fusion | flops 1310720 | bytes 1966080 | tf_op jit(solution)/shard_map/stack | solution.py:198
  4.8 2.3 %copy.49 = bf16[2,32,2560]{2,1,0:T(8,128)(2,1)} copy(bf16[2,32,2560]{1,2,0:T(8,128)(2,1)} %get-tuple-element.17) | data formatting | bytes 655360 | tf_op jit(solution)/shard_map/slice | solution.py:25
  7.1 12.4 %collective-permute-start.1 = (bf16[2,32,2560]{2,1,0:T(8,128)(2,1)}, bf16[2,32,2560]{2,1,0:T(8,128)(2,1)}, u32[]{:S(2)}, u32[]{:S(2)}) collective-permute-start(bf16[2,32,2560]{2,1,0:T(8,128)(2,1)} %copy.49), channel_id=1, source_target_pairs={{1,0},{2,1},{3,2},{4,3},{5,4},{6,5},{7,6},{8,7},{9,8},{10,9},{11,1... | collective-permute-start | bytes 983048 | tf_op jit(solution)/shard_map/ppermute | solution.py:25
  20.6 1.9 %collective-permute-start = (bf16[2,32,2560]{2,1,0:T(8,128)(2,1)}, bf16[2,32,2560]{2,1,0:T(8,128)(2,1)}, u32[]{:S(2)}, u32[]{:S(2)}) collective-permute-start(bf16[2,32,2560]{2,1,0:T(8,128)(2,1)} %copy.48), channel_id=1, source_target_pairs={{0,1},{1,2},{2,3},{3,4},{4,5},{5,6},{6,7},{7,8},{8,9},{9,10},{10,1... | collective-permute-start | bytes 983048 | tf_op jit(solution)/shard_map/ppermute | solution.py:22
  23.0 2.2 %copy.57 = bf16[1,128,2560]{1,2,0:T(8,128)(2,1)} copy(bf16[1,128,2560]{2,1,0:T(8,128)(2,1)} %param.9) | data formatting | bytes 1310720 | tf_op args[3]
  25.2 1.6 %collective-permute-done = bf16[2,32,2560]{2,1,0:T(8,128)(2,1)} collective-permute-done((bf16[2,32,2560]{2,1,0:T(8,128)(2,1)}, bf16[2,32,2560]{2,1,0:T(8,128)(2,1)}, u32[]{:S(2)}, u32[]{:S(2)}) %collective-permute-start) | collective-permute-done | bytes 327712 | tf_op jit(solution)/shard_map/ppermute | solution.py:22
  26.9 2.3 %copy.50 = bf16[2,32,2560]{1,2,0:T(8,128)(2,1)} copy(bf16[2,32,2560]{2,1,0:T(8,128)(2,1)} %collective-permute-done) | data formatting | bytes 655360 | tf_op jit(solution)/shard_map/ppermute | solution.py:22
  29.1 2.3 %copy.51 = bf16[2,32,2560]{1,2,0:T(8,128)(2,1)} copy(bf16[2,32,2560]{2,1,0:T(8,128)(2,1)} %collective-permute-done.1) | data formatting | bytes 655360 | tf_op jit(solution)/shard_map/ppermute | solution.py:25
  31.4 3.3 %pad_maximum_fusion = bf16[2,192,2560]{1,2,0:T(8,128)(2,1)S(1)} fusion(bf16[2,32,2560]{1,2,0:T(8,128)(2,1)} %copy.51, bf16[1,128,2560]{1,2,0:T(8,128)(2,1)S(1)} %copy.47, bf16[1,128,2560]{1,2,0:T(8,128)(2,1)S(1)} %copy-done.5, bf16[2,32,2560]{1,2,0:T(8,128)(2,1)} %copy.50), kind=kLoop, calls=%fused_computation.1 | loop fusion | flops 7864320 | bytes 3932160 | tf_op jit(solution)/shard_map/concatenate | solution.py:26
  36.4 1.9 %fusion.42 = (f32[20,128]{1,0:T(8,128)S(1)}, f32[20,128,192]{1,2,0:T(8,128)}) fusion(f32[20,128,192]{1,2,0:T(8,128)S(1)} %fusion.32, pred[192]{0:T(512)(128)(4,1)S(1)} %or_not_fusion), kind=kOutput, calls=%fused_computation.73 | output fusion | flops 1966271 | bytes 3942592 | tf_op jit(solution)/shard_map/sub | solution.py:153
  38.3 3.5 %fusion.8 = bf16[192,20,128]{2,0,1:T(8,128)(2,1)} fusion(bf16[128,20,128]{0,2,1:T(8,128)(2,1)} %bitcast.115, f32[20,128]{1,0:T(8,128)S(1)} %get-tuple-element.30, f32[20,128,192]{1,2,0:T(8,128)} %copy-done.3, pred[192]{0:T(512)(128)(4,1)S(1)} %or_not_fusion), kind=kOutput, calls=%fused_computation.18 | convolution fusion | flops 128780992 | bytes 3614912 | tf_op jit(solution)/shard_map/hqk,qhd->khd/dot_general | solution.py:175
  41.8 2.7 %fusion.26 = f32[128,20]{0,1:T(8,128)S(1)} fusion(bf16[192,20,128]{0,2,1:T(8,128)(2,1)S(1)} %bitcast.113, bf16[128,20,128]{0,2,1:T(8,128)(2,1)} %bitcast.116, f32[20,128]{1,0:T(8,128)S(1)} %get-tuple-element.30, f32[20,128,192]{1,2,0:T(8,128)} %copy-done.3, pred[192]{0:T(512)(128)(4,1)S(1)} %or_not_fusion), kind=kOutput, calls=%fused_computation.45 | convolution fusion | flops 129269952 | bytes 3625152 | tf_op jit(solution)/shard_map/hqk,khd->qhd/dot_general | solution.py:157
  44.4 2.5 %fusion.1 = bf16[20,128,192]{1,2,0:T(8,128)(2,1)S(1)} fusion(bf16[192,20,128]{0,2,1:T(8,128)(2,1)S(1)} %bitcast.114, bf16[128,20,128]{0,2,1:T(8,128)(2,1)} %bitcast.117, f32[20,128]{1,0:T(8,128)S(1)} %bitcast.122, f32[20,128,192]{1,2,0:T(8,128)} %get-tuple-element.31, f32[20,128]{1,0:T(8,128)S(1)} %get-tuple-element.30), kind=kOutput, calls=%fused_computation.3 | convolution fusion | flops 127795200 | bytes 4608000 | tf_op jit(solution)/shard_map/qhd,khd->hqk/dot_general | solution.py:161
  53.3 1.7 %copy.65 = f32[128,20,128]{0,2,1:T(8,128)S(1)} copy(f32[128,20,128]{2,0,1:T(8,128)} %slice_convert_fusion.1) | data formatting | bytes 2621440 | tf_op jit(solution)/shard_map/convert_element_type | solution.py:207
  58.6 2.8 %copy.73 = f32[128,20,128]{0,2,1:T(8,128)} copy(f32[128,20,128]{2,0,1:T(8,128)} %slice_convert_fusion) | data formatting | bytes 2621440 | tf_op jit(solution)/shard_map/convert_element_type | solution.py:208
  61.4 1.7 %pad_maximum_fusion.2 = bf16[2,32,2560]{2,1,0:T(8,128)(2,1)} fusion(bf16[1,32,2560]{2,1,0:T(8,128)(2,1)} %stack.33, bf16[1,32,2560]{2,1,0:T(8,128)(2,1)S(1)} %copy-done.10), kind=kLoop, calls=%fused_computation.54 | loop fusion | flops 163840 | bytes 655360 | tf_op jit(solution)/shard_map/stack | solution.py:211
  63.1 4.6 %collective-permute-start.2 = (bf16[2,32,2560]{2,1,0:T(8,128)(2,1)}, bf16[2,32,2560]{2,1,0:T(8,128)(2,1)}, u32[]{:S(2)}, u32[]{:S(2)}) collective-permute-start(bf16[2,32,2560]{2,1,0:T(8,128)(2,1)} %pad_maximum_fusion.2), channel_id=1, source_target_pairs={{0,1},{1,2},{2,3},{3,4},{4,5},{5,6},{6,7},{7,8},{8,9},{9,10},{10,1... | collective-permute-start | bytes 983048 | tf_op jit(solution)/shard_map/ppermute | solution.py:119
  67.6 1.5 %copy.63 = f32[128,2560]{1,0:T(8,128)} copy(f32[128,2560]{0,1:T(8,128)S(1)} %bitcast.102) | data formatting | bytes 2621440 | tf_op jit(solution)/shard_map/reshape | solution.py:181
  69.1 1.7 %fusion.25 = f32[128]{0:T(128)S(1)} fusion(f32[128,2560]{1,0:T(8,128)} %copy.63, bf16[1,128,2560]{2,1,0:T(8,128)(2,1)} %param.6, f32[2560]{0:T(1024)S(1)} %copy-done.12), kind=kLoop, calls=%fused_computation.42 | loop fusion | flops 1310592 | bytes 1976832 | tf_op jit(solution)/shard_map/reduce_sum | solution.py:131
  70.9 1.5 %copy.62 = f32[1,128,2560]{2,1,0:T(8,128)} copy(f32[1,128,2560]{1,2,0:T(8,128)S(1)} %bitcast.103) | data formatting | bytes 2621440 | tf_op jit(solution)/shard_map/reshape | solution.py:181
  72.3 2.9 %subtract_convert_fusion = bf16[1,128,2560]{2,1,0:T(8,128)(2,1)} fusion(f32[1,128,2560]{2,1,0:T(8,128)} %copy.62, bf16[1,128,2560]{2,1,0:T(8,128)(2,1)} %param.6, f32[128]{0:T(128)S(1)} %broadcast_multiply_fusion.1, f32[128]{0:T(128)S(1)} %get-tuple-element.28, f32[2560]{0:T(1024)S(1)} %copy-done.12, f32[128]{0:T(128)S(1)} %get-tuple-element.29), kind=kLoop, calls=%fused_computation.43 | loop fusion | flops 2293760 | bytes 2633216 | tf_op jit(solution)/shard_map/convert_element_type | solution.py:134
  76.0 1.9 %collective-permute-start.3 = (bf16[2,32,2560]{2,1,0:T(8,128)(2,1)}, bf16[2,32,2560]{2,1,0:T(8,128)(2,1)}, u32[]{:S(2)}, u32[]{:S(2)}) collective-permute-start(bf16[2,32,2560]{2,1,0:T(8,128)(2,1)} %pad_maximum_fusion.3), channel_id=1, source_target_pairs={{1,0},{2,1},{3,2},{4,3},{5,4},{6,5},{7,6},{8,7},{9,8},{10,9},{11,1... | collective-permute-start | bytes 983048 | tf_op jit(solution)/shard_map/ppermute | solution.py:119
  77.9 1.7 %fusion.40 = (bf16[1,32,2560]{2,1,0:T(8,128)(2,1)}, bf16[1,32,2560]{2,1,0:T(8,128)(2,1)S(1)}) fusion(bf16[2,32,2560]{2,1,0:T(8,128)(2,1)} %collective-permute-done.2), kind=kLoop, calls=%fused_computation.71 | loop fusion | bytes 655360 | tf_op jit(solution)/shard_map/slice | solution.py:222
  79.6 2.1 %copy.90 = bf16[1,32,2560]{1,2,0:T(8,128)(2,1)} copy(bf16[1,32,2560]{2,1,0:T(8,128)(2,1)} %get-tuple-element.22) | data formatting | bytes 327680
  81.7 3.0 %collective-permute-done.3 = bf16[2,32,2560]{2,1,0:T(8,128)(2,1)} collective-permute-done((bf16[2,32,2560]{2,1,0:T(8,128)(2,1)}, bf16[2,32,2560]{2,1,0:T(8,128)(2,1)}, u32[]{:S(2)}, u32[]{:S(2)}) %collective-permute-start.3) | collective-permute-done | bytes 327712 | tf_op jit(solution)/shard_map/ppermute | solution.py:119
  84.7 1.8 %fusion.41 = (bf16[1,32,2560]{2,1,0:T(8,128)(2,1)}, bf16[1,32,2560]{2,1,0:T(8,128)(2,1)}) fusion(bf16[2,32,2560]{2,1,0:T(8,128)(2,1)} %collective-permute-done.3), kind=kLoop, calls=%fused_computation.72 | loop fusion | bytes 655360 | tf_op jit(solution)/shard_map/slice | solution.py:223
  86.5 2.0 %copy.91 = bf16[1,32,2560]{1,2,0:T(8,128)(2,1)} copy(bf16[1,32,2560]{2,1,0:T(8,128)(2,1)} %get-tuple-element.24) | data formatting | bytes 327680
  88.4 2.6 %fusion.20 = bf16[128,2560]{0,1:T(8,128)(2,1)} fusion(f32[128,20,128]{0,2,1:T(8,128)S(1)} %copy-done.6, bf16[32,2560]{0,1:T(8,128)(2,1)} %bitcast.111, bf16[32,2560]{0,1:T(8,128)(2,1)} %bitcast.110), kind=kLoop, calls=%fused_computation.33 | loop fusion | flops 1638400 | bytes 2293760 | tf_op jit(solution)/shard_map/convert_element_type | solution.py:233
  91.1 2.2 %copy.77 = bf16[1,128,2560]{2,1,0:T(8,128)(2,1)} copy(bf16[1,128,2560]{1,2,0:T(8,128)(2,1)} %bitcast.112) | data formatting | bytes 1310720
  96.5 36.6 %shard_map.93 = f32[2,2560]{1,0:T(2,128)} custom-call(f32[2,2560]{1,0:T(2,128)} %pad_maximum_fusion.4.x_ref), custom_call_target="tpu_custom_call" | custom-call | tf_op jit(solution)/shard_map/pallas_call | solution.py:101
  133.2 1.5 %fusion.31 = bf16[1,128,2560]{1,2,0:T(8,128)(2,1)} fusion(bf16[1,128,2560]{1,2,0:T(8,128)(2,1)S(1)} %copy.46, f32[128]{0:T(128)S(1)} %broadcast_multiply_fusion, f32[128]{0:T(128)S(1)} %get-tuple-element.26, f32[2560]{0:T(1024)S(1)} %copy-done.13, f32[128]{0:T(128)S(1)} %get-tuple-element.27, bf16[32,2560]{0,1:T(8,128)(2,1)S(1)} %bitcast.109, ...), kind=kLoop, calls=%fused_computation.51 | loop fusion | flops 3604480 | bytes 2960896 | tf_op jit(solution)/shard_map/broadcast_in_dim | solution.py:232
  134.7 2.2 %copy.76 = bf16[1,128,2560]{2,1,0:T(8,128)(2,1)} copy(bf16[1,128,2560]{1,2,0:T(8,128)(2,1)} %fusion.31) | data formatting | bytes 1310720
  (68 shorter events, 20.4 us)
Async XLA Ops:
  0.6 1.9 %copy-start.11 = (bf16[1,128,2560]{2,1,0:T(8,128)(2,1)S(1)}, bf16[1,128,2560]{2,1,0:T(8,128)(2,1)}, u32[]{:S(2)}) copy-start(bf16[1,128,2560]{2,1,0:T(8,128)(2,1)} %param.8) | copy-start | bytes 1966084
  2.1 0.7 copy-start.13
  3.2 1.6 %copy-start.4 = (bf16[1,128,2560]{1,2,0:T(8,128)(2,1)}, bf16[1,128,2560]{1,2,0:T(8,128)(2,1)S(1)}, u32[]{:S(2)}) copy-start(bf16[1,128,2560]{1,2,0:T(8,128)(2,1)S(1)} %fusion.18) | copy-start | bytes 1966084
  4.8 17.8 %copy-start.2 = (bf16[1,128,2560]{2,1,0:T(8,128)(2,1)S(1)}, bf16[1,128,2560]{2,1,0:T(8,128)(2,1)}, u32[]{:S(2)}) copy-start(bf16[1,128,2560]{2,1,0:T(8,128)(2,1)} %param.6) | copy-start | bytes 1966084
  7.1 22.1 %collective-permute-start.1 = (bf16[2,32,2560]{2,1,0:T(8,128)(2,1)}, bf16[2,32,2560]{2,1,0:T(8,128)(2,1)}, u32[]{:S(2)}, u32[]{:S(2)}) collective-permute-start(bf16[2,32,2560]{2,1,0:T(8,128)(2,1)} %copy.49), channel_id=1, source_target_pairs={{1,0},{2,1},{3,2},{4,3},{5,4},{6,5},{7,6},{8,7},{9,8},{10,9},{11,1... | collective-permute-start | bytes 983048 | tf_op jit(solution)/shard_map/ppermute | solution.py:25
  20.6 6.2 %collective-permute-start = (bf16[2,32,2560]{2,1,0:T(8,128)(2,1)}, bf16[2,32,2560]{2,1,0:T(8,128)(2,1)}, u32[]{:S(2)}, u32[]{:S(2)}) collective-permute-start(bf16[2,32,2560]{2,1,0:T(8,128)(2,1)} %copy.48), channel_id=1, source_target_pairs={{0,1},{1,2},{2,3},{3,4},{4,5},{5,6},{6,7},{7,8},{8,9},{9,10},{10,1... | collective-permute-start | bytes 983048 | tf_op jit(solution)/shard_map/ppermute | solution.py:22
  25.2 6.2 %copy-start.5 = (bf16[1,128,2560]{1,2,0:T(8,128)(2,1)S(1)}, bf16[1,128,2560]{1,2,0:T(8,128)(2,1)}, u32[]{:S(2)}) copy-start(bf16[1,128,2560]{1,2,0:T(8,128)(2,1)} %copy-done.4) | copy-start | bytes 1966084
  34.7 0.7 copy-start.12
  34.9 1.5 %copy-start = (bf16[1,192,2560]{1,2,0:T(8,128)(2,1)}, bf16[1,192,2560]{1,2,0:T(8,128)(2,1)S(1)}, u32[]{:S(2)}) copy-start(bf16[1,192,2560]{1,2,0:T(8,128)(2,1)S(1)} %get-tuple-element.15) | copy-start | bytes 2949124
  36.4 1.9 %copy-start.3 = (f32[20,128,192]{1,2,0:T(8,128)}, f32[20,128,192]{1,2,0:T(8,128)S(1)}, u32[]{:S(2)}) copy-start(f32[20,128,192]{1,2,0:T(8,128)S(1)} %fusion.32) | copy-start | bytes 5898244
  44.4 2.5 %copy-start.1 = (bf16[1,192,2560]{1,2,0:T(8,128)(2,1)S(1)}, bf16[1,192,2560]{1,2,0:T(8,128)(2,1)}, u32[]{:S(2)}) copy-start(bf16[1,192,2560]{1,2,0:T(8,128)(2,1)} %copy-done) | copy-start | bytes 2949124
  48.2 1.5 %copy-start.7 = (bf16[192,20,128]{2,0,1:T(8,128)(2,1)S(1)}, bf16[192,20,128]{2,0,1:T(8,128)(2,1)}, u32[]{:S(2)}) copy-start(bf16[192,20,128]{2,0,1:T(8,128)(2,1)} %fusion.8) | copy-start | bytes 2949124
  58.6 2.8 %copy-start.10 = (bf16[1,32,2560]{2,1,0:T(8,128)(2,1)S(1)}, bf16[1,32,2560]{2,1,0:T(8,128)(2,1)}, u32[]{:S(2)}) copy-start(bf16[1,32,2560]{2,1,0:T(8,128)(2,1)} %stack.32) | copy-start | bytes 491524
  63.1 14.9 %collective-permute-start.2 = (bf16[2,32,2560]{2,1,0:T(8,128)(2,1)}, bf16[2,32,2560]{2,1,0:T(8,128)(2,1)}, u32[]{:S(2)}, u32[]{:S(2)}) collective-permute-start(bf16[2,32,2560]{2,1,0:T(8,128)(2,1)} %pad_maximum_fusion.2), channel_id=1, source_target_pairs={{0,1},{1,2},{2,3},{3,4},{4,5},{5,6},{6,7},{7,8},{8,9},{9,10},{10,1... | collective-permute-start | bytes 983048 | tf_op jit(solution)/shard_map/ppermute | solution.py:119
  72.3 2.9 %copy-start.8 = (bf16[1,32,2560]{2,1,0:T(8,128)(2,1)S(1)}, bf16[1,32,2560]{2,1,0:T(8,128)(2,1)}, u32[]{:S(2)}) copy-start(bf16[1,32,2560]{2,1,0:T(8,128)(2,1)} %stack.35) | copy-start | bytes 491524
  72.3 2.9 %copy-start.9 = (bf16[1,32,2560]{2,1,0:T(8,128)(2,1)S(1)}, bf16[1,32,2560]{2,1,0:T(8,128)(2,1)}, u32[]{:S(2)}) copy-start(bf16[1,32,2560]{2,1,0:T(8,128)(2,1)} %stack.36) | copy-start | bytes 491524
  76.0 8.7 %collective-permute-start.3 = (bf16[2,32,2560]{2,1,0:T(8,128)(2,1)}, bf16[2,32,2560]{2,1,0:T(8,128)(2,1)}, u32[]{:S(2)}, u32[]{:S(2)}) collective-permute-start(bf16[2,32,2560]{2,1,0:T(8,128)(2,1)} %pad_maximum_fusion.3), channel_id=1, source_target_pairs={{1,0},{2,1},{3,2},{4,3},{5,4},{6,5},{7,6},{8,7},{9,8},{10,9},{11,1... | collective-permute-start | bytes 983048 | tf_op jit(solution)/shard_map/ppermute | solution.py:119
  79.6 8.8 %copy-start.6 = (f32[128,20,128]{0,2,1:T(8,128)S(1)}, f32[128,20,128]{0,2,1:T(8,128)}, u32[]{:S(2)}) copy-start(f32[128,20,128]{0,2,1:T(8,128)} %copy.73) | copy-start | bytes 3932164
  134.7 2.2 %copy-start.14 = (f32[2,2560]{1,0:T(2,128)S(1)}, f32[2,2560]{1,0:T(2,128)}, u32[]{:S(2)}) copy-start(f32[2,2560]{1,0:T(2,128)} %shard_map.93) | copy-start | bytes 61444

commit v4 on v3

--- a/solution.py
+++ b/solution.py
@@ -192,17 +192,18 @@
     ctx_count = lax.axis_size("ctx")
     position = lax.axis_index("ctx")
     query_norm, query_factor = normalize(query_raw[0], query_gain)
-    key_norm, key_factor = normalize(key_raw[0], key_gain)
     own_values = value_rows[0]
     own_grads = out_grad[0]
-    key_window = padded(jnp.stack([key_norm, own_values]), (("ctx", 1),), margin)
+    key_window = padded(jnp.stack([key_raw[0], own_values]), (("ctx", 1),), margin)
+    window_keys, window_factor = normalize(key_window[0], key_gain)
+    key_factor = window_factor[margin : margin + tile_rows]
     slot_ids = jnp.arange(tile_rows + 2 * margin, dtype=jnp.int32)
     valid_keys = jnp.logical_not(
         (slot_ids < margin) & (position == 0)
         | (slot_ids >= margin + tile_rows) & (position == ctx_count - 1)
     )
     query_grad, key_terms, value_terms, log_total, row_delta = tile_pass(
-        query_norm, key_window[0], key_window[1], own_grads, valid_keys
+        query_norm, window_keys, key_window[1], own_grads, valid_keys
     )
     key_sum = key_terms[margin : margin + tile_rows].astype(jnp.float32)
     value_sum = value_terms[margin : margin + tile_rows].astype(jnp.float32)

time: 138 us -> 117 us (0.85)
  local copies, waits for them, and re-layouts: 40.7 us -> 30.5 us
  waiting for transfers between devices: 4.63 us -> 0.01 us
  other arithmetic: 23 us -> 18.8 us
  Pallas kernels: 36.6 us -> 35.2 us
    ppermute x2 -> x0, local copies, waits for them, and re-layouts: 4.53 us -> none  [the longest x1 2.27 us: padded(): lax.ppermute(lax.slice_in_dim(block, block.shape[dim] - width, None, axis...]
    ppermute x2, waiting for transfers between devices: 2.99 us -> 0.01 us  [shifted(): return lax.ppermute(block, axis, route)]
    convert_element_type x1 -> x2, local copies, waits for them, and re-layouts: 0.24 us -> 3 us  [normalize(): widened = raw_rows.astype(jnp.float32)]
    ppermute x1, starting transfers between devices: 1.91 us -> 4.49 us  [padded(): lax.ppermute(lax.slice_in_dim(block, block.shape[dim] - width, None, axis...]
    ppermute x1, starting transfers between devices: 12.4 us -> 9.89 us  [padded(): lax.ppermute(lax.slice_in_dim(block, 0, width, axis=dim), axis, backward)]
    slice x2 -> x1, local copies, waits for them, and re-layouts: 2.43 us -> 0.07 us  [per_device(): key_factor = window_factor[margin:margin + tile_rows]]
    reshape x2, local copies, waits for them, and re-layouts: 2.97 us -> 0.8 us  [tile_pass(): query_grad.reshape(query_rows.shape[0], flat_width)]
    concatenate x1, other arithmetic: 3.31 us -> 1.21 us  [padded(): block = jnp.concatenate([low, block, high], axis=dim)]
  transfers between devices with their start and end apart: 4 -> 4, of which waited for: 2 -> 0; matrix products, arithmetic and copies ran while one was open for 13% -> 12% of each run, Pallas kernels for 0% -> 0%
where the time goes in v4:
time: 117 us; the launch traced here: 116 us
  Pallas kernels  35.2 us (30%)
  local copies, waits for them, and re-layouts  30.5 us (26%)
  starting transfers between devices  19.6 us (17%)
  other arithmetic  18.8 us (16%)
  matrix products  10.7 us (9%)
    pallas_call x1, Pallas kernels, mesh_sum(): pl.pallas_call(functools.partial(sum_kernel, plan), out_shape=jax.ShapeDt...  35.2 us
    unnamed x35, local copies, waits for them, and re-layouts  16.6 us
    ppermute x1, starting transfers between devices, padded(): lax.ppermute(lax.slice_in_dim(block, 0, width, axis=dim), axis, backward)  9.89 us
    ppermute x2, starting transfers between devices, shifted(): return lax.ppermute(block, axis, route)  5.21 us
    ppermute x1, starting transfers between devices, padded(): lax.ppermute(lax.slice_in_dim(block, block.shape[dim] - width, None, axis...  4.49 us
    dot_general x1, matrix products, tile_pass(): jnp.einsum('hqk,qhd->khd', probs_half, grad_heads, preferred_element_type...  3.58 us
    convert_element_type x2, local copies, waits for them, and re-layouts, normalize(): widened = raw_rows.astype(jnp.float32)  3 us
    convert_element_type x1, other arithmetic, per_device(): value_sum.astype(jnp.bfloat16)[None]  2.91 us
  transfers between devices with their start and end apart: 4, of which 0 were waited for; matrix products, arithmetic and copies ran while one was open for 12% of the time, Pallas kernels for 0%

profile of v4, /device:TPU:1, one launch (start us, length us, event | category | flops | bytes accessed | tf_op | source)
XLA Modules:
  0.0 115.7 jit_solution(9369025883477162190)
XLA Ops:
  0.6 1.2 %constant_dynamic-update-slice_fusion.1 = bf16[2,128,2560]{2,1,0:T(8,128)(2,1)S(1)} fusion(bf16[1,128,2560]{2,1,0:T(8,128)(2,1)} %param.7), kind=kLoop, calls=%fused_computation.59 | loop fusion | bytes 1310720
  2.8 4.5 %collective-permute-start = (bf16[2,32,2560]{2,1,0:T(8,128)(2,1)}, bf16[2,32,2560]{2,1,0:T(8,128)(2,1)}, u32[]{:S(2)}, u32[]{:S(2)}) collective-permute-start(bf16[2,32,2560]{2,1,0:T(8,128)(2,1)} %get-tuple-element.16), channel_id=1, source_target_pairs={{0,1},{1,2},{2,3},{3,4},{4,5},{5,6},{6,7},{7,8},{8,9},{9,10},{10,1... | collective-permute-start | bytes 983048 | tf_op jit(solution)/shard_map/ppermute | solution.py:22
  7.3 9.9 %collective-permute-start.1 = (bf16[2,32,2560]{2,1,0:T(8,128)(2,1)}, bf16[2,32,2560]{2,1,0:T(8,128)(2,1)}, u32[]{:S(2)}, u32[]{:S(2)}) collective-permute-start(bf16[2,32,2560]{2,1,0:T(8,128)(2,1)} %get-tuple-element.17), channel_id=1, source_target_pairs={{1,0},{2,1},{3,2},{4,3},{5,4},{6,5},{7,6},{8,7},{9,8},{10,9},{11,1... | collective-permute-start | bytes 983048 | tf_op jit(solution)/shard_map/ppermute | solution.py:25
  17.7 2.2 %copy.63 = bf16[1,128,2560]{1,2,0:T(8,128)(2,1)} copy(bf16[1,128,2560]{2,1,0:T(8,128)(2,1)} %param.7) | data formatting | bytes 1310720 | tf_op args[1]
  19.9 2.2 %copy.47 = bf16[1,128,2560]{1,2,0:T(8,128)(2,1)} copy(bf16[1,128,2560]{2,1,0:T(8,128)(2,1)} %param.9) | data formatting | bytes 1310720 | tf_op args[3]
  22.1 1.2 %pad_maximum_fusion = bf16[2,192,2560]{2,1,0:T(8,128)(2,1)S(1)} fusion(bf16[2,32,2560]{2,1,0:T(8,128)(2,1)} %collective-permute-done.1, bf16[2,128,2560]{2,1,0:T(8,128)(2,1)S(1)} %constant_dynamic-update-slice_fusion, bf16[2,32,2560]{2,1,0:T(8,128)(2,1)} %collective-permute-done), kind=kLoop, calls=%fused_computation.2 | loop fusion | flops 5898240 | bytes 3932160 | tf_op jit(solution)/shard_map/concatenate | solution.py:26
  23.5 1.5 %slice_convert_fusion = (f32[1,192,2560]{2,1,0:T(8,128)}, bf16[1,192,2560]{2,1,0:T(8,128)(2,1)S(1)}) fusion(bf16[2,192,2560]{2,1,0:T(8,128)(2,1)S(1)} %pad_maximum_fusion), kind=kLoop, calls=%fused_computation.40 | loop fusion | flops 491520 | bytes 4915200 | tf_op jit(solution)/shard_map/convert_element_type | solution.py:123
  25.0 2.8 %reshape.208 = f32[192,20,128]{2,1,0:T(8,128)} reshape(f32[1,192,2560]{2,1,0:T(8,128)} %get-tuple-element.14) | data formatting | bytes 3932160 | tf_op jit(solution)/shard_map/convert_element_type | solution.py:123
  27.8 1.5 %reshape_squeeze.6 = bf16[192,20,128]{2,1,0:T(8,128)(2,1)} reshape(bf16[1,192,2560]{2,1,0:T(8,128)(2,1)S(1)} %get-tuple-element.15) | data formatting | bytes 1966080 | tf_op jit(solution)/shard_map/reshape;squeeze | solution.py:138
  29.3 2.0 %multiply_convert_fusion = bf16[192,20,128]{2,1,0:T(8,128)(2,1)S(1)} fusion(f32[192,20,128]{2,1,0:T(8,128)} %reshape.208, f32[20,128]{1,0:T(8,128)S(1)} %bitcast.94, f32[192]{0:T(256)S(1)} %add_rsqrt_fusion), kind=kLoop, calls=%fused_computation.1 | loop fusion | flops 1474560 | bytes 2960128 | tf_op jit(solution)/shard_map/convert_element_type | solution.py:125
  32.3 1.9 %fusion.40 = (f32[20,128]{1,0:T(8,128)S(1)}, f32[20,128,192]{1,2,0:T(8,128)}) fusion(f32[20,128,192]{1,2,0:T(8,128)S(1)} %fusion.24, pred[192]{0:T(512)(128)(4,1)S(1)} %or_not_fusion), kind=kOutput, calls=%fused_computation.75 | output fusion | flops 1966271 | bytes 3942592 | tf_op jit(solution)/shard_map/sub | solution.py:153
  34.2 3.6 %fusion.4 = bf16[192,20,128]{2,0,1:T(8,128)(2,1)} fusion(bf16[128,20,128]{0,2,1:T(8,128)(2,1)} %bitcast.89, f32[20,128]{1,0:T(8,128)S(1)} %get-tuple-element.28, f32[20,128,192]{1,2,0:T(8,128)} %copy-done.3, pred[192]{0:T(512)(128)(4,1)S(1)} %or_not_fusion), kind=kOutput, calls=%fused_computation.17 | convolution fusion | flops 128780992 | bytes 3614912 | tf_op jit(solution)/shard_map/hqk,qhd->khd/dot_general | solution.py:175
  37.8 2.8 %fusion.19 = f32[128,20]{0,1:T(8,128)S(1)} fusion(bf16[128,20,128]{0,2,1:T(8,128)(2,1)} %bitcast.90, bf16[192,20,128]{2,1,0:T(8,128)(2,1)S(1)} %copy-done.6, f32[20,128]{1,0:T(8,128)S(1)} %get-tuple-element.28, f32[20,128,192]{1,2,0:T(8,128)} %copy-done.3, pred[192]{0:T(512)(128)(4,1)S(1)} %or_not_fusion), kind=kOutput, calls=%fused_computation.39 | convolution fusion | flops 129269952 | bytes 3625152 | tf_op jit(solution)/shard_map/hqk,khd->qhd/dot_general | solution.py:157
  40.6 2.3 %fusion.1 = bf16[20,128,192]{1,2,0:T(8,128)(2,1)S(1)} fusion(bf16[128,20,128]{0,2,1:T(8,128)(2,1)} %bitcast.91, f32[20,128]{1,0:T(8,128)S(1)} %bitcast.97, f32[20,128,192]{1,2,0:T(8,128)} %get-tuple-element.29, f32[20,128]{1,0:T(8,128)S(1)} %get-tuple-element.28, bf16[192,20,128]{2,1,0:T(8,128)(2,1)S(1)} %copy-done.6), kind=kOutput, calls=%fused_computation.7 | convolution fusion | flops 127795200 | bytes 4608000 | tf_op jit(solution)/shard_map/qhd,khd->hqk/dot_general | solution.py:161
  43.5 1.2 %slice_convert_fusion.2 = f32[128,20,128]{2,0,1:T(8,128)} fusion(bf16[192,20,128]{2,0,1:T(8,128)(2,1)S(1)} %fusion.5), kind=kLoop, calls=%fused_computation.53 | loop fusion | flops 327680 | bytes 1966080 | tf_op jit(solution)/shard_map/convert_element_type | solution.py:208
  46.2 1.0 fusion.37
  48.2 1.9 %collective-permute-start.2 = (bf16[2,32,2560]{2,1,0:T(8,128)(2,1)}, bf16[2,32,2560]{2,1,0:T(8,128)(2,1)}, u32[]{:S(2)}, u32[]{:S(2)}) collective-permute-start(bf16[2,32,2560]{2,1,0:T(8,128)(2,1)} %pad_maximum_fusion.1), channel_id=1, source_target_pairs={{0,1},{1,2},{2,3},{3,4},{4,5},{5,6},{6,7},{7,8},{8,9},{9,10},{10,1... | collective-permute-start | bytes 983048 | tf_op jit(solution)/shard_map/ppermute | solution.py:119
  51.2 3.3 %collective-permute-start.3 = (bf16[2,32,2560]{2,1,0:T(8,128)(2,1)}, bf16[2,32,2560]{2,1,0:T(8,128)(2,1)}, u32[]{:S(2)}, u32[]{:S(2)}) collective-permute-start(bf16[2,32,2560]{2,1,0:T(8,128)(2,1)} %pad_maximum_fusion.2), channel_id=1, source_target_pairs={{1,0},{2,1},{3,2},{4,3},{5,4},{6,5},{7,6},{8,7},{9,8},{10,9},{11,1... | collective-permute-start | bytes 983048 | tf_op jit(solution)/shard_map/ppermute | solution.py:119
  55.6 1.4 %subtract_convert_fusion = bf16[1,128,2560]{2,1,0:T(8,128)(2,1)} fusion(f32[1,128,2560]{2,1,0:T(8,128)S(1)} %copy.52, bf16[1,128,2560]{2,1,0:T(8,128)(2,1)S(1)} %copy-done, f32[128]{0:T(128)S(1)} %broadcast_multiply_fusion.1, f32[128]{0:T(128)S(1)} %get-tuple-element.26, f32[2560]{0:T(1024)S(1)} %copy-done.9, f32[128]{0:T(128)S(1)} %get-tuple-element.27), kind=kLoop, calls=%fused_computation.37 | loop fusion | flops 2293760 | bytes 2633216 | tf_op jit(solution)/shard_map/convert_element_type | solution.py:134
  57.0 1.2 %slice_convert_fusion.1 = f32[128,20,128]{2,0,1:T(8,128)} fusion(bf16[192,20,128]{2,0,1:T(8,128)(2,1)S(1)} %copy-done.7), kind=kLoop, calls=%fused_computation.52 | loop fusion | flops 327680 | bytes 1966080 | tf_op jit(solution)/shard_map/convert_element_type | solution.py:209
  59.2 2.8 %copy.64 = f32[128,20,128]{0,2,1:T(8,128)} copy(f32[128,20,128]{2,0,1:T(8,128)} %slice_convert_fusion.1) | data formatting | bytes 2621440 | tf_op jit(solution)/shard_map/convert_element_type | solution.py:209
  62.1 1.0 fusion.38
  63.4 1.7 %fusion.39 = (bf16[1,32,2560]{2,1,0:T(8,128)(2,1)}, bf16[1,32,2560]{2,1,0:T(8,128)(2,1)}) fusion(bf16[2,32,2560]{2,1,0:T(8,128)(2,1)} %collective-permute-done.3), kind=kLoop, calls=%fused_computation.74 | loop fusion | bytes 655360 | tf_op jit(solution)/shard_map/slice | solution.py:224
  65.2 1.2 %copy.74 = bf16[1,32,2560]{1,2,0:T(8,128)(2,1)S(1)} copy(bf16[1,32,2560]{2,1,0:T(8,128)(2,1)} %get-tuple-element.25) | data formatting | bytes 327680
  66.4 1.1 fusion.11
  68.1 35.2 %shard_map.93 = f32[2,2560]{1,0:T(2,128)} custom-call(f32[2,2560]{1,0:T(2,128)} %pad_maximum_fusion.3.x_ref), custom_call_target="tpu_custom_call" | custom-call | tf_op jit(solution)/shard_map/pallas_call | solution.py:101
  103.3 1.1 copy.75
  104.4 2.0 %copy.76 = bf16[1,32,2560]{1,2,0:T(8,128)(2,1)} copy(bf16[1,32,2560]{2,1,0:T(8,128)(2,1)} %get-tuple-element.24) | data formatting | bytes 327680
  106.4 2.9 %fusion.13 = bf16[128,2560]{0,1:T(8,128)(2,1)} fusion(f32[128,20,128]{0,2,1:T(8,128)} %copy.64, bf16[32,2560]{0,1:T(8,128)(2,1)} %bitcast.87, bf16[32,2560]{0,1:T(8,128)(2,1)} %bitcast.86), kind=kLoop, calls=%fused_computation.27 | loop fusion | flops 1638400 | bytes 2293760 | tf_op jit(solution)/shard_map/convert_element_type | solution.py:234
  109.3 2.2 %copy.68 = bf16[1,128,2560]{2,1,0:T(8,128)(2,1)} copy(bf16[1,128,2560]{1,2,0:T(8,128)(2,1)} %bitcast.88) | data formatting | bytes 1310720
  111.5 1.5 %fusion.29 = bf16[1,128,2560]{1,2,0:T(8,128)(2,1)} fusion(bf16[1,128,2560]{1,2,0:T(8,128)(2,1)S(1)} %copy-done.4, f32[128]{0:T(128)S(1)} %broadcast_multiply_fusion, f32[128]{0:T(128)S(1)} %fusion.30, f32[2560]{0:T(1024)S(1)} %copy-done.10, f32[128]{0:T(128)S(1)} %slice.58, bf16[32,2560]{0,1:T(8,128)(2,1)S(1)} %bitcast.85, bf16[32,2560]{0,1:T(8,128)(2,1)S(1)} %bitcast.83, ...), kind=kLoop, calls=%fused_computation.51 | loop fusion | flops 3604480 | bytes 2960896 | tf_op jit(solution)/shard_map/broadcast_in_dim | solution.py:233
  112.9 2.2 %copy.67 = bf16[1,128,2560]{2,1,0:T(8,128)(2,1)} copy(bf16[1,128,2560]{1,2,0:T(8,128)(2,1)} %fusion.29) | data formatting | bytes 1310720
  (63 shorter events, 10.6 us)
Async XLA Ops:
  0.6 1.3 %copy-start.8 = (bf16[1,128,2560]{2,1,0:T(8,128)(2,1)S(1)}, bf16[1,128,2560]{2,1,0:T(8,128)(2,1)}, u32[]{:S(2)}) copy-start(bf16[1,128,2560]{2,1,0:T(8,128)(2,1)} %param.8) | copy-start | bytes 1966084
  1.9 15.3 %copy-start = (bf16[1,128,2560]{2,1,0:T(8,128)(2,1)S(1)}, bf16[1,128,2560]{2,1,0:T(8,128)(2,1)}, u32[]{:S(2)}) copy-start(bf16[1,128,2560]{2,1,0:T(8,128)(2,1)} %param.6) | copy-start | bytes 1966084
  2.8 19.2 %collective-permute-start = (bf16[2,32,2560]{2,1,0:T(8,128)(2,1)}, bf16[2,32,2560]{2,1,0:T(8,128)(2,1)}, u32[]{:S(2)}, u32[]{:S(2)}) collective-permute-start(bf16[2,32,2560]{2,1,0:T(8,128)(2,1)} %get-tuple-element.16), channel_id=1, source_target_pairs={{0,1},{1,2},{2,3},{3,4},{4,5},{5,6},{6,7},{7,8},{8,9},{9,10},{10,1... | collective-permute-start | bytes 983048 | tf_op jit(solution)/shard_map/ppermute | solution.py:22
  7.3 14.7 %collective-permute-start.1 = (bf16[2,32,2560]{2,1,0:T(8,128)(2,1)}, bf16[2,32,2560]{2,1,0:T(8,128)(2,1)}, u32[]{:S(2)}, u32[]{:S(2)}) collective-permute-start(bf16[2,32,2560]{2,1,0:T(8,128)(2,1)} %get-tuple-element.17), channel_id=1, source_target_pairs={{1,0},{2,1},{3,2},{4,3},{5,4},{6,5},{7,6},{8,7},{9,8},{10,9},{11,1... | collective-permute-start | bytes 983048 | tf_op jit(solution)/shard_map/ppermute | solution.py:25
  27.8 1.5 %copy-start.10 = (f32[2560]{0:T(1024)S(1)}, f32[2560]{0:T(1024)}, u32[]{:S(2)}) copy-start(f32[2560]{0:T(1024)} %param.11) | copy-start | bytes 30724
  29.3 2.0 %copy-start.9 = (f32[2560]{0:T(1024)S(1)}, f32[2560]{0:T(1024)}, u32[]{:S(2)}) copy-start(f32[2560]{0:T(1024)} %param.10) | copy-start | bytes 30724
  31.3 1.0 copy-start.1
  32.3 1.9 %copy-start.3 = (f32[20,128,192]{1,2,0:T(8,128)}, f32[20,128,192]{1,2,0:T(8,128)S(1)}, u32[]{:S(2)}) copy-start(f32[20,128,192]{1,2,0:T(8,128)S(1)} %fusion.24) | copy-start | bytes 5898244
  34.2 3.6 %copy-start.6 = (bf16[192,20,128]{2,1,0:T(8,128)(2,1)S(1)}, bf16[192,20,128]{2,1,0:T(8,128)(2,1)}, u32[]{:S(2)}) copy-start(bf16[192,20,128]{2,1,0:T(8,128)(2,1)} %reshape_squeeze.6) | copy-start | bytes 2949124
  43.5 1.7 %copy-start.2 = (bf16[192,20,128]{2,1,0:T(8,128)(2,1)S(1)}, bf16[192,20,128]{2,1,0:T(8,128)(2,1)}, u32[]{:S(2)}) copy-start(bf16[192,20,128]{2,1,0:T(8,128)(2,1)} %copy-done.1) | copy-start | bytes 2949124
  48.2 13.9 %collective-permute-start.2 = (bf16[2,32,2560]{2,1,0:T(8,128)(2,1)}, bf16[2,32,2560]{2,1,0:T(8,128)(2,1)}, u32[]{:S(2)}, u32[]{:S(2)}) collective-permute-start(bf16[2,32,2560]{2,1,0:T(8,128)(2,1)} %pad_maximum_fusion.1), channel_id=1, source_target_pairs={{0,1},{1,2},{2,3},{3,4},{4,5},{5,6},{6,7},{7,8},{8,9},{9,10},{10,1... | collective-permute-start | bytes 983048 | tf_op jit(solution)/shard_map/ppermute | solution.py:119
  51.2 12.2 %collective-permute-start.3 = (bf16[2,32,2560]{2,1,0:T(8,128)(2,1)}, bf16[2,32,2560]{2,1,0:T(8,128)(2,1)}, u32[]{:S(2)}, u32[]{:S(2)}) collective-permute-start(bf16[2,32,2560]{2,1,0:T(8,128)(2,1)} %pad_maximum_fusion.2), channel_id=1, source_target_pairs={{1,0},{2,1},{3,2},{4,3},{5,4},{6,5},{7,6},{8,7},{9,8},{10,9},{11,1... | collective-permute-start | bytes 983048 | tf_op jit(solution)/shard_map/ppermute | solution.py:119
  55.6 1.4 %copy-start.7 = (bf16[192,20,128]{2,0,1:T(8,128)(2,1)S(1)}, bf16[192,20,128]{2,0,1:T(8,128)(2,1)}, u32[]{:S(2)}) copy-start(bf16[192,20,128]{2,0,1:T(8,128)(2,1)} %fusion.4) | copy-start | bytes 2949124
  57.0 1.8 %copy-start.5 = (f32[128,20,128]{2,0,1:T(8,128)S(1)}, f32[128,20,128]{2,0,1:T(8,128)}, u32[]{:S(2)}) copy-start(f32[128,20,128]{2,0,1:T(8,128)} %slice_convert_fusion.2) | copy-start | bytes 3932164
  63.1 3.3 %copy-start.4 = (bf16[1,128,2560]{1,2,0:T(8,128)(2,1)S(1)}, bf16[1,128,2560]{1,2,0:T(8,128)(2,1)}, u32[]{:S(2)}) copy-start(bf16[1,128,2560]{1,2,0:T(8,128)(2,1)} %copy.63) | copy-start | bytes 1966084
  112.9 2.2 %copy-start.11 = (f32[2,2560]{1,0:T(2,128)S(1)}, f32[2,2560]{1,0:T(2,128)}, u32[]{:S(2)}) copy-start(f32[2,2560]{1,0:T(2,128)} %shard_map.93) | copy-start | bytes 61444

commit v5 on v4

--- a/solution.py
+++ b/solution.py
@@ -28,7 +28,7 @@
 
 
 AXIS_PARTS = {"ctx": (4, 4, 2), "dp": (8, 3)}
-SUM_ORDER = (("dp", 1), ("dp", 0), ("ctx", 0), ("ctx", 1), ("ctx", 2))
+SUM_ORDER = (("ctx", 2), ("ctx", 1), ("ctx", 0), ("dp", 0), ("dp", 1))
 
 
 def sum_plan():

time: 117 us -> 115 us (0.983)
  the two profiles are of different devices: /device:TPU:1 before, /device:TPU:4 now
where the time goes in v5:
time: 115 us; the launch traced here: 114 us
  Pallas kernels  41.6 us (36%)
  local copies, waits for them, and re-layouts  30.5 us (27%)
  other arithmetic  18.8 us (16%)
  starting transfers between devices  11.4 us (10%)
  matrix products  10.7 us (9%)
    pallas_call x1, Pallas kernels, mesh_sum(): pl.pallas_call(functools.partial(sum_kernel, plan), out_shape=jax.ShapeDt...  41.6 us
    unnamed x35, local copies, waits for them, and re-layouts  16.6 us
    ppermute x2, starting transfers between devices, shifted(): return lax.ppermute(block, axis, route)  5.89 us
    ppermute x1, starting transfers between devices, padded(): lax.ppermute(lax.slice_in_dim(block, 0, width, axis=dim), axis, backward)  3.64 us
    dot_general x1, matrix products, tile_pass(): jnp.einsum('hqk,qhd->khd', probs_half, grad_heads, preferred_element_type...  3.58 us
    convert_element_type x2, local copies, waits for them, and re-layouts, normalize(): widened = raw_rows.astype(jnp.float32)  3 us
    convert_element_type x1, other arithmetic, per_device(): value_sum.astype(jnp.bfloat16)[None]  2.91 us
    convert_element_type x1, local copies, waits for them, and re-layouts, per_device(): value_sum = value_terms[margin:margin + tile_rows].astype(jnp.float32)  2.78 us
  transfers between devices with their start and end apart: 4, of which 1 were waited for; matrix products, arithmetic and copies ran while one was open for 12% of the time, Pallas kernels for 0%

profile of v5, /device:TPU:4, one launch (start us, length us, event | category | flops | bytes accessed | tf_op | source)
XLA Modules:
  0.0 114.0 jit_solution(5009129808577332286)
XLA Ops:
  0.6 1.2 %constant_dynamic-update-slice_fusion.1 = bf16[2,128,2560]{2,1,0:T(8,128)(2,1)S(1)} fusion(bf16[1,128,2560]{2,1,0:T(8,128)(2,1)} %param.7), kind=kLoop, calls=%fused_computation.59 | loop fusion | bytes 1310720
  2.8 1.9 %collective-permute-start = (bf16[2,32,2560]{2,1,0:T(8,128)(2,1)}, bf16[2,32,2560]{2,1,0:T(8,128)(2,1)}, u32[]{:S(2)}, u32[]{:S(2)}) collective-permute-start(bf16[2,32,2560]{2,1,0:T(8,128)(2,1)} %get-tuple-element.16), channel_id=1, source_target_pairs={{0,1},{1,2},{2,3},{3,4},{4,5},{5,6},{6,7},{7,8},{8,9},{9,10},{10,1... | collective-permute-start | bytes 983048 | tf_op jit(solution)/shard_map/ppermute | solution.py:22
  4.7 3.6 %collective-permute-start.1 = (bf16[2,32,2560]{2,1,0:T(8,128)(2,1)}, bf16[2,32,2560]{2,1,0:T(8,128)(2,1)}, u32[]{:S(2)}, u32[]{:S(2)}) collective-permute-start(bf16[2,32,2560]{2,1,0:T(8,128)(2,1)} %get-tuple-element.17), channel_id=1, source_target_pairs={{1,0},{2,1},{3,2},{4,3},{5,4},{6,5},{7,6},{8,7},{9,8},{10,9},{11,1... | collective-permute-start | bytes 983048 | tf_op jit(solution)/shard_map/ppermute | solution.py:25
  8.9 2.2 %copy.63 = bf16[1,128,2560]{1,2,0:T(8,128)(2,1)} copy(bf16[1,128,2560]{2,1,0:T(8,128)(2,1)} %param.7) | data formatting | bytes 1310720 | tf_op args[1]
  11.0 2.2 %copy.47 = bf16[1,128,2560]{1,2,0:T(8,128)(2,1)} copy(bf16[1,128,2560]{2,1,0:T(8,128)(2,1)} %param.9) | data formatting | bytes 1310720 | tf_op args[3]
  13.3 1.2 %pad_maximum_fusion = bf16[2,192,2560]{2,1,0:T(8,128)(2,1)S(1)} fusion(bf16[2,32,2560]{2,1,0:T(8,128)(2,1)} %collective-permute-done.1, bf16[2,128,2560]{2,1,0:T(8,128)(2,1)S(1)} %constant_dynamic-update-slice_fusion, bf16[2,32,2560]{2,1,0:T(8,128)(2,1)} %collective-permute-done), kind=kLoop, calls=%fused_computation.2 | loop fusion | flops 5898240 | bytes 3932160 | tf_op jit(solution)/shard_map/concatenate | solution.py:26
  14.8 1.5 %slice_convert_fusion = (f32[1,192,2560]{2,1,0:T(8,128)}, bf16[1,192,2560]{2,1,0:T(8,128)(2,1)S(1)}) fusion(bf16[2,192,2560]{2,1,0:T(8,128)(2,1)S(1)} %pad_maximum_fusion), kind=kLoop, calls=%fused_computation.40 | loop fusion | flops 491520 | bytes 4915200 | tf_op jit(solution)/shard_map/convert_element_type | solution.py:123
  16.3 2.8 %reshape.208 = f32[192,20,128]{2,1,0:T(8,128)} reshape(f32[1,192,2560]{2,1,0:T(8,128)} %get-tuple-element.14) | data formatting | bytes 3932160 | tf_op jit(solution)/shard_map/convert_element_type | solution.py:123
  19.0 1.5 %reshape_squeeze.6 = bf16[192,20,128]{2,1,0:T(8,128)(2,1)} reshape(bf16[1,192,2560]{2,1,0:T(8,128)(2,1)S(1)} %get-tuple-element.15) | data formatting | bytes 1966080 | tf_op jit(solution)/shard_map/reshape;squeeze | solution.py:138
  20.5 2.0 %multiply_convert_fusion = bf16[192,20,128]{2,1,0:T(8,128)(2,1)S(1)} fusion(f32[192,20,128]{2,1,0:T(8,128)} %reshape.208, f32[20,128]{1,0:T(8,128)S(1)} %bitcast.94, f32[192]{0:T(256)S(1)} %add_rsqrt_fusion), kind=kLoop, calls=%fused_computation.1 | loop fusion | flops 1474560 | bytes 2960128 | tf_op jit(solution)/shard_map/convert_element_type | solution.py:125
  23.5 1.9 %fusion.40 = (f32[20,128]{1,0:T(8,128)S(1)}, f32[20,128,192]{1,2,0:T(8,128)}) fusion(f32[20,128,192]{1,2,0:T(8,128)S(1)} %fusion.24, pred[192]{0:T(512)(128)(4,1)S(1)} %or_not_fusion), kind=kOutput, calls=%fused_computation.75 | output fusion | flops 1966271 | bytes 3942592 | tf_op jit(solution)/shard_map/sub | solution.py:153
  25.4 3.6 %fusion.4 = bf16[192,20,128]{2,0,1:T(8,128)(2,1)} fusion(bf16[128,20,128]{0,2,1:T(8,128)(2,1)} %bitcast.89, f32[20,128]{1,0:T(8,128)S(1)} %get-tuple-element.28, f32[20,128,192]{1,2,0:T(8,128)} %copy-done.3, pred[192]{0:T(512)(128)(4,1)S(1)} %or_not_fusion), kind=kOutput, calls=%fused_computation.17 | convolution fusion | flops 128780992 | bytes 3614912 | tf_op jit(solution)/shard_map/hqk,qhd->khd/dot_general | solution.py:175
  29.0 2.8 %fusion.19 = f32[128,20]{0,1:T(8,128)S(1)} fusion(bf16[128,20,128]{0,2,1:T(8,128)(2,1)} %bitcast.90, bf16[192,20,128]{2,1,0:T(8,128)(2,1)S(1)} %copy-done.6, f32[20,128]{1,0:T(8,128)S(1)} %get-tuple-element.28, f32[20,128,192]{1,2,0:T(8,128)} %copy-done.3, pred[192]{0:T(512)(128)(4,1)S(1)} %or_not_fusion), kind=kOutput, calls=%fused_computation.39 | convolution fusion | flops 129269952 | bytes 3625152 | tf_op jit(solution)/shard_map/hqk,khd->qhd/dot_general | solution.py:157
  31.8 2.3 %fusion.1 = bf16[20,128,192]{1,2,0:T(8,128)(2,1)S(1)} fusion(bf16[128,20,128]{0,2,1:T(8,128)(2,1)} %bitcast.91, f32[20,128]{1,0:T(8,128)S(1)} %bitcast.97, f32[20,128,192]{1,2,0:T(8,128)} %get-tuple-element.29, f32[20,128]{1,0:T(8,128)S(1)} %get-tuple-element.28, bf16[192,20,128]{2,1,0:T(8,128)(2,1)S(1)} %copy-done.6), kind=kOutput, calls=%fused_computation.7 | convolution fusion | flops 127795200 | bytes 4608000 | tf_op jit(solution)/shard_map/qhd,khd->hqk/dot_general | solution.py:161
  34.8 1.2 %slice_convert_fusion.2 = f32[128,20,128]{2,0,1:T(8,128)} fusion(bf16[192,20,128]{2,0,1:T(8,128)(2,1)S(1)} %fusion.5), kind=kLoop, calls=%fused_computation.53 | loop fusion | flops 327680 | bytes 1966080 | tf_op jit(solution)/shard_map/convert_element_type | solution.py:208
  37.4 1.0 fusion.37
  39.4 3.4 %collective-permute-start.2 = (bf16[2,32,2560]{2,1,0:T(8,128)(2,1)}, bf16[2,32,2560]{2,1,0:T(8,128)(2,1)}, u32[]{:S(2)}, u32[]{:S(2)}) collective-permute-start(bf16[2,32,2560]{2,1,0:T(8,128)(2,1)} %pad_maximum_fusion.1), channel_id=1, source_target_pairs={{0,1},{1,2},{2,3},{3,4},{4,5},{5,6},{6,7},{7,8},{8,9},{9,10},{10,1... | collective-permute-start | bytes 983048 | tf_op jit(solution)/shard_map/ppermute | solution.py:119
  43.9 2.5 %collective-permute-start.3 = (bf16[2,32,2560]{2,1,0:T(8,128)(2,1)}, bf16[2,32,2560]{2,1,0:T(8,128)(2,1)}, u32[]{:S(2)}, u32[]{:S(2)}) collective-permute-start(bf16[2,32,2560]{2,1,0:T(8,128)(2,1)} %pad_maximum_fusion.2), channel_id=1, source_target_pairs={{1,0},{2,1},{3,2},{4,3},{5,4},{6,5},{7,6},{8,7},{9,8},{10,9},{11,1... | collective-permute-start | bytes 983048 | tf_op jit(solution)/shard_map/ppermute | solution.py:119
  47.5 1.4 %subtract_convert_fusion = bf16[1,128,2560]{2,1,0:T(8,128)(2,1)} fusion(f32[1,128,2560]{2,1,0:T(8,128)S(1)} %copy.52, bf16[1,128,2560]{2,1,0:T(8,128)(2,1)S(1)} %copy-done, f32[128]{0:T(128)S(1)} %broadcast_multiply_fusion.1, f32[128]{0:T(128)S(1)} %get-tuple-element.26, f32[2560]{0:T(1024)S(1)} %copy-done.9, f32[128]{0:T(128)S(1)} %get-tuple-element.27), kind=kLoop, calls=%fused_computation.37 | loop fusion | flops 2293760 | bytes 2633216 | tf_op jit(solution)/shard_map/convert_element_type | solution.py:134
  48.9 1.2 %slice_convert_fusion.1 = f32[128,20,128]{2,0,1:T(8,128)} fusion(bf16[192,20,128]{2,0,1:T(8,128)(2,1)S(1)} %copy-done.7), kind=kLoop, calls=%fused_computation.52 | loop fusion | flops 327680 | bytes 1966080 | tf_op jit(solution)/shard_map/convert_element_type | solution.py:209
  51.1 2.8 %copy.64 = f32[128,20,128]{0,2,1:T(8,128)} copy(f32[128,20,128]{2,0,1:T(8,128)} %slice_convert_fusion.1) | data formatting | bytes 2621440 | tf_op jit(solution)/shard_map/convert_element_type | solution.py:209
  54.0 1.0 fusion.38
  55.3 1.7 %fusion.39 = (bf16[1,32,2560]{2,1,0:T(8,128)(2,1)}, bf16[1,32,2560]{2,1,0:T(8,128)(2,1)}) fusion(bf16[2,32,2560]{2,1,0:T(8,128)(2,1)} %collective-permute-done.3), kind=kLoop, calls=%fused_computation.74 | loop fusion | bytes 655360 | tf_op jit(solution)/shard_map/slice | solution.py:224
  57.1 1.2 %copy.74 = bf16[1,32,2560]{1,2,0:T(8,128)(2,1)S(1)} copy(bf16[1,32,2560]{2,1,0:T(8,128)(2,1)} %get-tuple-element.25) | data formatting | bytes 327680
  58.3 1.1 fusion.11
  60.0 41.6 %shard_map.93 = f32[2,2560]{1,0:T(2,128)} custom-call(f32[2,2560]{1,0:T(2,128)} %pad_maximum_fusion.3.x_ref), custom_call_target="tpu_custom_call" | custom-call | tf_op jit(solution)/shard_map/pallas_call | solution.py:101
  101.6 1.1 copy.75
  102.7 2.0 %copy.76 = bf16[1,32,2560]{1,2,0:T(8,128)(2,1)} copy(bf16[1,32,2560]{2,1,0:T(8,128)(2,1)} %get-tuple-element.24) | data formatting | bytes 327680
  104.7 2.9 %fusion.13 = bf16[128,2560]{0,1:T(8,128)(2,1)} fusion(f32[128,20,128]{0,2,1:T(8,128)} %copy.64, bf16[32,2560]{0,1:T(8,128)(2,1)} %bitcast.87, bf16[32,2560]{0,1:T(8,128)(2,1)} %bitcast.86), kind=kLoop, calls=%fused_computation.27 | loop fusion | flops 1638400 | bytes 2293760 | tf_op jit(solution)/shard_map/convert_element_type | solution.py:234
  107.6 2.2 %copy.68 = bf16[1,128,2560]{2,1,0:T(8,128)(2,1)} copy(bf16[1,128,2560]{1,2,0:T(8,128)(2,1)} %bitcast.88) | data formatting | bytes 1310720
  109.8 1.5 %fusion.29 = bf16[1,128,2560]{1,2,0:T(8,128)(2,1)} fusion(bf16[1,128,2560]{1,2,0:T(8,128)(2,1)S(1)} %copy-done.4, f32[128]{0:T(128)S(1)} %broadcast_multiply_fusion, f32[128]{0:T(128)S(1)} %fusion.30, f32[2560]{0:T(1024)S(1)} %copy-done.10, f32[128]{0:T(128)S(1)} %slice.58, bf16[32,2560]{0,1:T(8,128)(2,1)S(1)} %bitcast.85, bf16[32,2560]{0,1:T(8,128)(2,1)S(1)} %bitcast.83, ...), kind=kLoop, calls=%fused_computation.51 | loop fusion | flops 3604480 | bytes 2960896 | tf_op jit(solution)/shard_map/broadcast_in_dim | solution.py:233
  111.2 2.2 %copy.67 = bf16[1,128,2560]{2,1,0:T(8,128)(2,1)} copy(bf16[1,128,2560]{1,2,0:T(8,128)(2,1)} %fusion.29) | data formatting | bytes 1310720
  (63 shorter events, 10.7 us)
Async XLA Ops:
  0.6 1.3 %copy-start.8 = (bf16[1,128,2560]{2,1,0:T(8,128)(2,1)S(1)}, bf16[1,128,2560]{2,1,0:T(8,128)(2,1)}, u32[]{:S(2)}) copy-start(bf16[1,128,2560]{2,1,0:T(8,128)(2,1)} %param.8) | copy-start | bytes 1966084
  1.9 6.5 %copy-start = (bf16[1,128,2560]{2,1,0:T(8,128)(2,1)S(1)}, bf16[1,128,2560]{2,1,0:T(8,128)(2,1)}, u32[]{:S(2)}) copy-start(bf16[1,128,2560]{2,1,0:T(8,128)(2,1)} %param.6) | copy-start | bytes 1966084
  2.8 10.4 %collective-permute-start = (bf16[2,32,2560]{2,1,0:T(8,128)(2,1)}, bf16[2,32,2560]{2,1,0:T(8,128)(2,1)}, u32[]{:S(2)}, u32[]{:S(2)}) collective-permute-start(bf16[2,32,2560]{2,1,0:T(8,128)(2,1)} %get-tuple-element.16), channel_id=1, source_target_pairs={{0,1},{1,2},{2,3},{3,4},{4,5},{5,6},{6,7},{7,8},{8,9},{9,10},{10,1... | collective-permute-start | bytes 983048 | tf_op jit(solution)/shard_map/ppermute | solution.py:22
  4.7 8.5 %collective-permute-start.1 = (bf16[2,32,2560]{2,1,0:T(8,128)(2,1)}, bf16[2,32,2560]{2,1,0:T(8,128)(2,1)}, u32[]{:S(2)}, u32[]{:S(2)}) collective-permute-start(bf16[2,32,2560]{2,1,0:T(8,128)(2,1)} %get-tuple-element.17), channel_id=1, source_target_pairs={{1,0},{2,1},{3,2},{4,3},{5,4},{6,5},{7,6},{8,7},{9,8},{10,9},{11,1... | collective-permute-start | bytes 983048 | tf_op jit(solution)/shard_map/ppermute | solution.py:25
  19.0 1.5 %copy-start.10 = (f32[2560]{0:T(1024)S(1)}, f32[2560]{0:T(1024)}, u32[]{:S(2)}) copy-start(f32[2560]{0:T(1024)} %param.11) | copy-start | bytes 30724
  20.5 2.0 %copy-start.9 = (f32[2560]{0:T(1024)S(1)}, f32[2560]{0:T(1024)}, u32[]{:S(2)}) copy-start(f32[2560]{0:T(1024)} %param.10) | copy-start | bytes 30724
  22.5 1.0 copy-start.1
  23.5 1.9 %copy-start.3 = (f32[20,128,192]{1,2,0:T(8,128)}, f32[20,128,192]{1,2,0:T(8,128)S(1)}, u32[]{:S(2)}) copy-start(f32[20,128,192]{1,2,0:T(8,128)S(1)} %fusion.24) | copy-start | bytes 5898244
  25.4 3.6 %copy-start.6 = (bf16[192,20,128]{2,1,0:T(8,128)(2,1)S(1)}, bf16[192,20,128]{2,1,0:T(8,128)(2,1)}, u32[]{:S(2)}) copy-start(bf16[192,20,128]{2,1,0:T(8,128)(2,1)} %reshape_squeeze.6) | copy-start | bytes 2949124
  34.7 1.7 %copy-start.2 = (bf16[192,20,128]{2,1,0:T(8,128)(2,1)S(1)}, bf16[192,20,128]{2,1,0:T(8,128)(2,1)}, u32[]{:S(2)}) copy-start(bf16[192,20,128]{2,1,0:T(8,128)(2,1)} %copy-done.1) | copy-start | bytes 2949124
  39.4 14.6 %collective-permute-start.2 = (bf16[2,32,2560]{2,1,0:T(8,128)(2,1)}, bf16[2,32,2560]{2,1,0:T(8,128)(2,1)}, u32[]{:S(2)}, u32[]{:S(2)}) collective-permute-start(bf16[2,32,2560]{2,1,0:T(8,128)(2,1)} %pad_maximum_fusion.1), channel_id=1, source_target_pairs={{0,1},{1,2},{2,3},{3,4},{4,5},{5,6},{6,7},{7,8},{8,9},{9,10},{10,1... | collective-permute-start | bytes 983048 | tf_op jit(solution)/shard_map/ppermute | solution.py:119
  43.9 11.4 %collective-permute-start.3 = (bf16[2,32,2560]{2,1,0:T(8,128)(2,1)}, bf16[2,32,2560]{2,1,0:T(8,128)(2,1)}, u32[]{:S(2)}, u32[]{:S(2)}) collective-permute-start(bf16[2,32,2560]{2,1,0:T(8,128)(2,1)} %pad_maximum_fusion.2), channel_id=1, source_target_pairs={{1,0},{2,1},{3,2},{4,3},{5,4},{6,5},{7,6},{8,7},{9,8},{10,9},{11,1... | collective-permute-start | bytes 983048 | tf_op jit(solution)/shard_map/ppermute | solution.py:119
  47.5 1.4 %copy-start.7 = (bf16[192,20,128]{2,0,1:T(8,128)(2,1)S(1)}, bf16[192,20,128]{2,0,1:T(8,128)(2,1)}, u32[]{:S(2)}) copy-start(bf16[192,20,128]{2,0,1:T(8,128)(2,1)} %fusion.4) | copy-start | bytes 2949124
  48.9 1.8 %copy-start.5 = (f32[128,20,128]{2,0,1:T(8,128)S(1)}, f32[128,20,128]{2,0,1:T(8,128)}, u32[]{:S(2)}) copy-start(f32[128,20,128]{2,0,1:T(8,128)} %slice_convert_fusion.2) | copy-start | bytes 3932164
  55.0 3.3 %copy-start.4 = (bf16[1,128,2560]{1,2,0:T(8,128)(2,1)S(1)}, bf16[1,128,2560]{1,2,0:T(8,128)(2,1)}, u32[]{:S(2)}) copy-start(bf16[1,128,2560]{1,2,0:T(8,128)(2,1)} %copy.63) | copy-start | bytes 1966084
  111.2 2.2 %copy-start.11 = (f32[2,2560]{1,0:T(2,128)S(1)}, f32[2,2560]{1,0:T(2,128)}, u32[]{:S(2)}) copy-start(f32[2,2560]{1,0:T(2,128)} %shard_map.93) | copy-start | bytes 61444
